TPU v7x, 256 devices: a whole 4x4x8 slice. The times are simulated.
256 devices in a mesh: die: 2 (over z_lo), row: 16 (over z_hi, x), col: 8 (over y, core).
Axes of the slice: x: 4, y: 4, z: 8 (z_hi: 4, z_lo: 2; z = z_hi * 2 + z_lo), core: 2. Of those that a mesh axis runs over, the one named last changes fastest.
Arguments:
- old_voltage: float32 [2, 4, 2048, 8192], P(None, 'die', 'row', 'col'), may hold values from 0 to 1
- capacitance: float32 [2, 4, 2048, 8192], P(None, 'die', 'row', 'col'), may hold values from 1 to 4
- east_conductance: float32 [2, 4, 2048, 8192], P(None, 'die', 'row', 'col'), may hold values from 0.25 to 2
- south_conductance: float32 [2, 4, 2048, 8192], P(None, 'die', 'row', 'col'), may hold values from 0.25 to 2
- through_vias: int32 [4, 16, 8, 32], P('die', 'row', 'col'), may hold values from 0 to 511, all different within a row
- via_conductance: float32 [2, 4, 16, 8, 32], P(None, 'die', 'row', 'col'), may hold values from 1 to 8
- load_patterns: int32 [4, 128, 512], P('die', 'row', 'col'), may hold values from 0 to 15
- pattern_currents: float32 [16, 256], replicated, may hold values from 0 to 4
Outputs:
- voltage: float32 [2, 4, 2048, 8192], P(None, 'die', 'row', 'col')
Inputs may be any that keep to these rules, and one draw needn't show every extreme that they name: `through_vias`: the 32 entries of one tile of one die are different block numbers.
All inputs are finite; a program needn't handle non-finite values.
Results may differ from a plain program's by a relative error of at most 0.00005.
Values sent between devices are 32-bit elements; how exact they have to be, the bound alone decides.
A program may use at most 64 MiB of HBM per device.

v0:
```python
import jax
import jax.numpy as jnp
from jax import lax
from jax.sharding import PartitionSpec as P

BS = 16


sweep_weights = (0.85, 1.35)
highest = lax.Precision.HIGHEST


def shifted(block, axis, distance):
    devices = range(lax.axis_size(axis))
    route = [(i - distance, i) for i in devices if i - distance in devices]
    return lax.ppermute(block, axis, route)


def with_halo(block, sides, width):
    for axis, dim in sides:
        count = lax.axis_size(axis)
        forward = [(i, i + 1) for i in range(count - 1)]
        backward = [(target, source) for source, target in forward]
        low = lax.ppermute(
            lax.slice_in_dim(block, block.shape[dim] - width, None, axis=dim), axis, forward
        )
        high = lax.ppermute(lax.slice_in_dim(block, 0, width, axis=dim), axis, backward)
        block = jnp.concatenate([low, block, high], axis=dim)
    return block


def center_columns(block_cols, block):
    columns = jnp.arange(block_cols * block)
    return (columns[None, :] == jnp.arange(block_cols)[:, None] * block + block // 2).astype(
        jnp.float32
    )


def place_centers(values, block):
    leading = values.shape[:-2]
    block_rows = values.shape[-2]
    block_cols = values.shape[-1]
    selector = center_columns(block_cols, block)
    spread = jnp.einsum("...rb,bj->...rj", values, selector, precision=highest)
    marker = (jnp.arange(block) == block // 2).astype(jnp.float32)
    placed = spread[..., :, None, :] * marker[:, None]
    return placed.reshape(leading + (block_rows * block, block_cols * block))


def block_currents(load_patterns, pattern_currents, block):
    layers, block_rows, block_cols = load_patterns.shape
    patterns = pattern_currents.shape[0]
    columns = jnp.arange(block_cols * block)
    owner = (columns[None, :] // block == jnp.arange(block_cols)[:, None]).astype(jnp.float32)
    within = (columns[None, :] % block == jnp.arange(block)[:, None]).astype(jnp.float32)
    picks = (load_patterns[..., None] == jnp.arange(patterns)).astype(jnp.float32)
    chosen = jnp.einsum("dibp,bj->dipj", picks, owner, precision=highest)
    laid = jnp.einsum(
        "pab,bj->paj", pattern_currents.reshape(patterns, block, block), within, precision=highest
    )
    cells = jnp.sum(chosen[:, :, :, None, :] * laid[None, None], axis=2)
    return cells.reshape(layers, block_rows * block, block_cols * block)


def local(
    old_voltage,
    capacitance,
    east_conductance,
    south_conductance,
    through_vias,
    via_conductance,
    load_patterns,
    pattern_currents,
):
    nets, layers, rows_here, cols_here = old_voltage.shape
    block = BS
    block_rows = rows_here // block
    block_cols = cols_here // block
    blocks_all = block_rows * block_cols
    col_final = lax.axis_index("col") == lax.axis_size("col") - 1
    row_final = lax.axis_index("row") == lax.axis_size("row") - 1
    col_keep = jnp.logical_not(
        jnp.logical_and(col_final, jnp.arange(cols_here) == cols_here - 1)
    ).astype(jnp.float32)
    row_keep = jnp.logical_not(
        jnp.logical_and(row_final, jnp.arange(rows_here) == rows_here - 1)
    ).astype(jnp.float32)[:, None]
    east = east_conductance * col_keep
    south = south_conductance * row_keep
    west_edge = shifted(east[..., -1], "col", 1)
    north_edge = shifted(south[..., -1, :], "row", 1)
    west = jnp.concatenate([west_edge[..., None], east[..., :-1]], axis=3)
    north = jnp.concatenate([north_edge[..., None, :], south[..., :-1, :]], axis=2)
    via_sites = through_vias.reshape(layers, -1)
    via_values = via_conductance.reshape(nets, layers, -1)
    onehot = (via_sites[..., None] == jnp.arange(blocks_all)).astype(jnp.float32)
    down_blocks = jnp.einsum("ndk,dkb->ndb", via_values, onehot, precision=highest)
    sites_above = shifted(via_sites[0], "die", -1)
    values_above = shifted(via_values[:, 0], "die", -1)
    onehot_above = (sites_above[:, None] == jnp.arange(blocks_all)).astype(jnp.float32)
    top_up = jnp.einsum("nk,kb->nb", values_above, onehot_above, precision=highest)
    up_blocks = jnp.concatenate([down_blocks[:, 1:], top_up[:, None]], axis=1)
    via_down = place_centers(down_blocks.reshape(nets, layers, block_rows, block_cols), block)
    via_up = place_centers(up_blocks.reshape(nets, layers, block_rows, block_cols), block)
    current = block_currents(load_patterns, pattern_currents, block)
    net_sign = jnp.array([-1.0, 1.0], jnp.float32).reshape(2, 1, 1, 1)
    supply = jnp.array([1.0, 0.0], jnp.float32).reshape(2, 1, 1, 1)
    die_first = lax.axis_index("die") * layers
    ground = (die_first + jnp.arange(layers) == 0).astype(jnp.float32).reshape(1, layers, 1, 1)
    rhs = capacitance * old_voltage + net_sign * current[None] + ground * supply * via_down
    diagonal = capacitance + east + west + south + north + via_down + via_up
    volts = old_voltage
    for weight_now in sweep_weights:
        padded = with_halo(volts, (("row", 2), ("col", 3)), 1)
        beside = (
            east * padded[:, :, 1:-1, 2:]
            + west * padded[:, :, 1:-1, :-2]
            + south * padded[:, :, 2:, 1:-1]
            + north * padded[:, :, :-2, 1:-1]
        )
        lower_top = shifted(volts[:, layers - 1], "die", 1)
        upper_bottom = shifted(volts[:, 0], "die", -1)
        below = jnp.concatenate([lower_top[:, None], volts[:, :-1]], axis=1)
        above = jnp.concatenate([volts[:, 1:], upper_bottom[:, None]], axis=1)
        vertical = via_down * below + via_up * above
        applied = diagonal * volts - beside - vertical
        volts = volts + weight_now * (rhs - applied) / diagonal
    return volts


def solution(mesh):
    in_specs = (
        P(None, "die", "row", "col"),
        P(None, "die", "row", "col"),
        P(None, "die", "row", "col"),
        P(None, "die", "row", "col"),
        P("die", "row", "col", None),
        P(None, "die", "row", "col", None),
        P("die", "row", "col"),
        P(),
    )
    out_specs = P(None, "die", "row", "col")
    return jax.shard_map(local, mesh=mesh, in_specs=in_specs, out_specs=out_specs, check_vma=False)
```

profile of v0, /device:TPU:110, one launch (start us, length us, event | category | flops | bytes accessed | tf_op | source)
XLA Modules:
  0.0 138.6 jit_solution(3489568064367580684)
XLA Ops:
  0.0 1.9 %copy_multiply_fusion.2 = f32[2,2,128,1024]{3,2,0,1:T(8,128)S(1)} fusion(f32[2,2,128,1024]{3,2,1,0:T(8,128)} %param.12, f32[1024]{0:T(1024)S(1)} %fusion.57), kind=kLoop, calls=%fused_computation.62 | loop fusion | flops 524288 | bytes 4198400 | tf_op jit(solution)/shard_map/mul | solution.py:88
  3.6 1.9 %collective-permute-start = (f32[2,2,128]{2,1,0:T(2,128)S(1)}, f32[2,2,128]{2,1,0:T(2,128)S(1)}, u32[]{:S(2)}, u32[]{:S(2)}) collective-permute-start(f32[2,2,128]{2,1,0:T(2,128)S(1)} %bitcast.84), channel_id=1, source_target_pairs={{0,1},{1,2},{2,3},{3,4},{4,5},{5,6},{6,7},{8,9},{9,10},{10,11},{11... | collective-permute-start | bytes 6152 | tf_op jit(solution)/shard_map/ppermute | solution.py:16
  5.5 2.0 %copy_multiply_fusion.1 = f32[2,2,128,1024]{3,2,0,1:T(8,128)S(1)} fusion(f32[2,2,128,1024]{3,2,1,0:T(8,128)} %param.13, f32[128]{0:T(128)S(1)} %not_convert_fusion), kind=kLoop, calls=%fused_computation.57 | loop fusion | flops 524288 | bytes 4194816 | tf_op jit(solution)/shard_map/mul | solution.py:89
  9.5 5.4 %collective-permute-start.1 = (f32[2,2,1024]{2,0,1:T(2,128)}, f32[2,2,1024]{2,0,1:T(2,128)}, u32[]{:S(2)}, u32[]{:S(2)}) collective-permute-start(f32[2,2,1024]{2,0,1:T(2,128)} %bitcast.70), channel_id=1, source_target_pairs={{0,8},{8,16},{16,24},{24,32},{32,40},{40,48},{48,56},{56,64},{64,7... | collective-permute-start | bytes 49160 | tf_op jit(solution)/shard_map/ppermute | solution.py:16
  14.9 2.9 %collective-permute-start.3 = (f32[2,32]{1,0:T(2,128)S(1)}, f32[2,32]{1,0:T(2,128)S(1)}, u32[]{:S(2)}, u32[]{:S(2)}) collective-permute-start(f32[2,32]{1,0:T(2,128)S(1)} %bitcast.85), channel_id=1, source_target_pairs={{128,0},{129,1},{130,2},{131,3},{132,4},{133,5},{134,6},{135,7},{1... | collective-permute-start | bytes 776 | tf_op jit(solution)/shard_map/ppermute | solution.py:16
  19.8 3.4 %collective-permute-start.4 = (f32[2,2,1,1024]{3,2,0,1:T(1,128)}, f32[2,2,1,1024]{3,2,0,1:T(1,128)}, u32[]{:S(2)}, u32[]{:S(2)}) collective-permute-start(f32[2,2,1,1024]{3,2,0,1:T(1,128)} %get-tuple-element.20), channel_id=1, source_target_pairs={{0,8},{8,16},{16,24},{24,32},{32,40},{40,48},{48,56},{56,64},{64,7... | collective-permute-start | bytes 49160 | tf_op jit(solution)/shard_map/ppermute | solution.py:24
  23.5 2.3 %fusion.61 = (f32[2,1,128,1024]{3,2,0,1:T(8,128)}, f32[2,128,1024]{2,1,0:T(8,128)}, f32[2,128,1024]{2,1,0:T(8,128)}, f32[2,1,128,1024]{3,2,0,1:T(8,128)}) fusion(f32[2,2,128,1024]{3,2,1,0:T(8,128)S(1)} %copy-done), kind=kLoop, calls=%fused_computation.124 | loop fusion | bytes 6291456 | tf_op jit(solution)/shard_map/slice | solution.py:121
  28.9 1.7 %multiply_reduce_fusion = f32[2,8,16,1024]{3,2,1,0:T(8,128)S(1)} fusion(f32[16,16,1024]{2,1,0:T(8,128)S(1)} %convolution_bitcast_fusion, f32[2,8,16,1024]{3,2,1,0:T(8,128)S(1)} %fusion.31), kind=kLoop, calls=%fused_computation | loop fusion | flops 8126464 | bytes 3145728 | tf_op jit(solution)/shard_map/reduce_sum | solution.py:61
  31.9 6.6 %collective-permute-start.9 = (f32[2,128,1024]{2,1,0:T(8,128)}, f32[2,128,1024]{2,1,0:T(8,128)}, u32[]{:S(2)}, u32[]{:S(2)}) collective-permute-start(f32[2,128,1024]{2,1,0:T(8,128)} %get-tuple-element.17), channel_id=1, source_target_pairs={{128,0},{129,1},{130,2},{131,3},{132,4},{133,5},{134,6},{135,7},{1... | collective-permute-start | bytes 3145736 | tf_op jit(solution)/shard_map/ppermute | solution.py:16
  38.8 2.4 %collective-permute-start.5 = (f32[2,2,1,1024]{3,2,0,1:T(1,128)}, f32[2,2,1,1024]{3,2,0,1:T(1,128)}, u32[]{:S(2)}, u32[]{:S(2)}) collective-permute-start(f32[2,2,1,1024]{3,2,0,1:T(1,128)} %get-tuple-element.19), channel_id=1, source_target_pairs={{8,0},{16,8},{24,16},{32,24},{40,32},{48,40},{56,48},{64,56},{72,6... | collective-permute-start | bytes 49160 | tf_op jit(solution)/shard_map/ppermute | solution.py:27
  43.9 19.7 %collective-permute-done.5 = f32[2,2,1,1024]{3,2,0,1:T(1,128)} collective-permute-done((f32[2,2,1,1024]{3,2,0,1:T(1,128)}, f32[2,2,1,1024]{3,2,0,1:T(1,128)}, u32[]{:S(2)}, u32[]{:S(2)}) %collective-permute-start.5) | collective-permute-done | bytes 16416 | tf_op jit(solution)/shard_map/ppermute | solution.py:27
  64.4 1.9 %collective-permute-start.6 = (f32[2,2,130,1]{3,2,0,1:T(8,128)S(1)}, f32[2,2,130,1]{3,2,0,1:T(8,128)S(1)}, u32[]{:S(2)}, u32[]{:S(2)}) collective-permute-start(f32[2,2,130,1]{3,2,0,1:T(8,128)S(1)} %get-tuple-element.7), channel_id=1, source_target_pairs={{1,0},{2,1},{3,2},{4,3},{5,4},{6,5},{7,6},{9,8},{10,9},{11,10},{12... | collective-permute-start | bytes 6248 | tf_op jit(solution)/shard_map/ppermute | solution.py:27
  66.3 2.4 %collective-permute-start.7 = (f32[2,2,130,1]{3,2,0,1:T(8,128)S(1)}, f32[2,2,130,1]{3,2,0,1:T(8,128)S(1)}, u32[]{:S(2)}, u32[]{:S(2)}) collective-permute-start(f32[2,2,130,1]{3,2,0,1:T(8,128)S(1)} %get-tuple-element.8), channel_id=1, source_target_pairs={{0,1},{1,2},{2,3},{3,4},{4,5},{5,6},{6,7},{8,9},{9,10},{10,11},{11... | collective-permute-start | bytes 6248 | tf_op jit(solution)/shard_map/ppermute | solution.py:24
  68.8 4.5 %fusion.19 = (f32[2,2,128,1024]{3,2,0,1:T(8,128)S(1)}, f32[2,2,128,1024]{3,2,0,1:T(8,128)S(1)}, f32[2,2,128,1024]{3,2,0,1:T(8,128)S(1)}) fusion(f32[128]{0:T(128)S(1)} %mul.198, f32[2,2,8,1024]{3,2,0,1:T(8,128)S(1)} %fusion.36, f32[2,2]{0,1:T(2,128)S(1)} %broadcast_multiply_fusion, f32[2,2,127,1024]{3,2,0,1:T(8,128)} %bitcast.76, ...), kind=kLoop, calls=%fused_computation.44 | loop fusion | flops 6291456 | bytes 17044496 | tf_op jit(solution)/shard_map/mul | solution.py:110
  77.1 6.7 %fusion.10 = f32[2,2,128,1024]{3,2,0,1:T(8,128)S(1)} fusion(f32[2,2,128,1024]{3,2,0,1:T(8,128)S(1)} %copy-done.10, f32[2,2,1,1024]{3,2,0,1:T(1,128)} %collective-permute-done.4, f32[2,2,1,1024]{3,2,0,1:T(1,128)} %collective-permute-done.5, f32[2,2,130,1]{3,2,0,1:T(8,128)} %copy-done.14, f32[2,2,130,1]{3,2,0,1:T(8,128)} %copy-done.13, ...), kind=kLoop, calls=%fused_computation.20 | loop fusion | flops 15204352 | bytes 19178560 | tf_op jit(solution)/shard_map/sub | solution.py:126
  89.1 6.6 %collective-permute-start.15 = (f32[2,128,1024]{2,1,0:T(8,128)S(1)}, f32[2,128,1024]{2,1,0:T(8,128)}, u32[]{:S(2)}, u32[]{:S(2)}) collective-permute-start(f32[2,128,1024]{2,1,0:T(8,128)S(1)} %get-tuple-element.13), channel_id=1, source_target_pairs={{128,0},{129,1},{130,2},{131,3},{132,4},{133,5},{134,6},{135,7},{1... | collective-permute-start | bytes 3145736 | tf_op jit(solution)/shard_map/ppermute | solution.py:16
  95.7 1.9 %collective-permute-start.10 = (f32[2,2,1,1024]{3,2,0,1:T(1,128)S(1)}, f32[2,2,1,1024]{3,2,0,1:T(1,128)S(1)}, u32[]{:S(2)}, u32[]{:S(2)}) collective-permute-start(f32[2,2,1,1024]{3,2,0,1:T(1,128)S(1)} %get-tuple-element.10), channel_id=1, source_target_pairs={{0,8},{8,16},{16,24},{24,32},{32,40},{40,48},{48,56},{56,64},{64,7... | collective-permute-start | bytes 49160 | tf_op jit(solution)/shard_map/ppermute | solution.py:24
  97.7 3.9 %collective-permute-start.11 = (f32[2,2,1,1024]{3,2,0,1:T(1,128)S(1)}, f32[2,2,1,1024]{3,2,0,1:T(1,128)S(1)}, u32[]{:S(2)}, u32[]{:S(2)}) collective-permute-start(f32[2,2,1,1024]{3,2,0,1:T(1,128)S(1)} %get-tuple-element.9), channel_id=1, source_target_pairs={{8,0},{16,8},{24,16},{32,24},{40,32},{48,40},{56,48},{64,56},{72,6... | collective-permute-start | bytes 49160 | tf_op jit(solution)/shard_map/ppermute | solution.py:27
  101.6 16.9 %collective-permute-done.11 = f32[2,2,1,1024]{3,2,0,1:T(1,128)S(1)} collective-permute-done((f32[2,2,1,1024]{3,2,0,1:T(1,128)S(1)}, f32[2,2,1,1024]{3,2,0,1:T(1,128)S(1)}, u32[]{:S(2)}, u32[]{:S(2)}) %collective-permute-start.11) | collective-permute-done | bytes 16416 | tf_op jit(solution)/shard_map/ppermute | solution.py:27
  118.7 2.2 %collective-permute-start.12 = (f32[2,2,130,1]{3,2,0,1:T(8,128)S(1)}, f32[2,2,130,1]{3,2,0,1:T(8,128)S(1)}, u32[]{:S(2)}, u32[]{:S(2)}) collective-permute-start(f32[2,2,130,1]{3,2,0,1:T(8,128)S(1)} %get-tuple-element.5), channel_id=1, source_target_pairs={{1,0},{2,1},{3,2},{4,3},{5,4},{6,5},{7,6},{9,8},{10,9},{11,10},{12... | collective-permute-start | bytes 6248 | tf_op jit(solution)/shard_map/ppermute | solution.py:27
  120.9 2.1 %collective-permute-start.13 = (f32[2,2,130,1]{3,2,0,1:T(8,128)S(1)}, f32[2,2,130,1]{3,2,0,1:T(8,128)S(1)}, u32[]{:S(2)}, u32[]{:S(2)}) collective-permute-start(f32[2,2,130,1]{3,2,0,1:T(8,128)S(1)} %get-tuple-element.6), channel_id=1, source_target_pairs={{0,1},{1,2},{2,3},{3,4},{4,5},{5,6},{6,7},{8,9},{9,10},{10,11},{11... | collective-permute-start | bytes 6248 | tf_op jit(solution)/shard_map/ppermute | solution.py:24
  123.1 1.9 %collective-permute-done.12 = f32[2,2,130,1]{3,2,0,1:T(8,128)S(1)} collective-permute-done((f32[2,2,130,1]{3,2,0,1:T(8,128)S(1)}, f32[2,2,130,1]{3,2,0,1:T(8,128)S(1)}, u32[]{:S(2)}, u32[]{:S(2)}) %collective-permute-start.12) | collective-permute-done | bytes 2112 | tf_op jit(solution)/shard_map/ppermute | solution.py:27
  125.0 3.8 %collective-permute-done.13 = f32[2,2,130,1]{3,2,0,1:T(8,128)S(1)} collective-permute-done((f32[2,2,130,1]{3,2,0,1:T(8,128)S(1)}, f32[2,2,130,1]{3,2,0,1:T(8,128)S(1)}, u32[]{:S(2)}, u32[]{:S(2)}) %collective-permute-start.13) | collective-permute-done | bytes 2112 | tf_op jit(solution)/shard_map/ppermute | solution.py:24
  129.5 9.1 %fusion.23 = f32[2,2,128,1024]{3,2,1,0:T(8,128)} fusion(f32[2,2,128,1024]{3,2,1,0:T(8,128)S(1)} %copy_add_fusion, f32[2,2,128,1024]{3,2,0,1:T(8,128)} %copy-done.8, f32[2,128,1024]{2,1,0:T(8,128)S(1)} %bitcast.80, f32[2]{0:T(128)S(1)} %copy-done.20, f32[2,2,128,1024]{3,2,1,0:T(8,128)} %param.11, f32[2,2,128,1024]{3,2,1,0:T(8,128)S(1)} %copy-done, ...), kind=kLoop, calls=%fused_computation.49 | loop fusion | flops 21495808 | bytes 28615752 | tf_op jit(solution)/shard_map/add | solution.py:127
  (101 shorter events, 23.8 us)
Async XLA Ops:
  3.6 35.2 %collective-permute-start = (f32[2,2,128]{2,1,0:T(2,128)S(1)}, f32[2,2,128]{2,1,0:T(2,128)S(1)}, u32[]{:S(2)}, u32[]{:S(2)}) collective-permute-start(f32[2,2,128]{2,1,0:T(2,128)S(1)} %bitcast.84), channel_id=1, source_target_pairs={{0,1},{1,2},{2,3},{3,4},{4,5},{5,6},{6,7},{8,9},{9,10},{10,11},{11... | collective-permute-start | bytes 6152 | tf_op jit(solution)/shard_map/ppermute | solution.py:16
  5.5 9.4 %copy-start.21 = (f32[2,2,1,1,32]{4,3,2,1,0:T(1,128)S(1)}, f32[2,2,1,1,32]{4,3,2,1,0:T(1,128)}, u32[]{:S(2)}) copy-start(f32[2,2,1,1,32]{4,3,2,1,0:T(1,128)} %param.15) | copy-start | bytes 1540
  5.5 12.3 %copy-start.23 = (s32[2,1,1,32]{3,2,1,0:T(1,128)S(1)}, s32[2,1,1,32]{3,2,1,0:T(1,128)}, u32[]{:S(2)}) copy-start(s32[2,1,1,32]{3,2,1,0:T(1,128)} %param.14) | copy-start | bytes 772
  5.5 13.6 %copy-start = (f32[2,2,128,1024]{3,2,1,0:T(8,128)S(1)}, f32[2,2,128,1024]{3,2,1,0:T(8,128)}, u32[]{:S(2)}) copy-start(f32[2,2,128,1024]{3,2,1,0:T(8,128)} %param.10) | copy-start | bytes 6291460
  9.5 33.5 %collective-permute-start.1 = (f32[2,2,1024]{2,0,1:T(2,128)}, f32[2,2,1024]{2,0,1:T(2,128)}, u32[]{:S(2)}, u32[]{:S(2)}) collective-permute-start(f32[2,2,1024]{2,0,1:T(2,128)} %bitcast.70), channel_id=1, source_target_pairs={{0,8},{8,16},{16,24},{24,32},{32,40},{40,48},{48,56},{56,64},{64,7... | collective-permute-start | bytes 49160 | tf_op jit(solution)/shard_map/ppermute | solution.py:16
  14.9 17.0 %collective-permute-start.3 = (f32[2,32]{1,0:T(2,128)S(1)}, f32[2,32]{1,0:T(2,128)S(1)}, u32[]{:S(2)}, u32[]{:S(2)}) collective-permute-start(f32[2,32]{1,0:T(2,128)S(1)} %bitcast.85), channel_id=1, source_target_pairs={{128,0},{129,1},{130,2},{131,3},{132,4},{133,5},{134,6},{135,7},{1... | collective-permute-start | bytes 776 | tf_op jit(solution)/shard_map/ppermute | solution.py:16
  17.9 12.8 %collective-permute-start.2 = (s32[32]{0:T(128)S(1)}, s32[32]{0:T(128)S(1)}, u32[]{:S(2)}, u32[]{:S(2)}) collective-permute-start(s32[32]{0:T(128)S(1)} %slice_bitcast_fusion.2), channel_id=1, source_target_pairs={{128,0},{129,1},{130,2},{131,3},{132,4},{133,5},{134,6},{135,7},{1... | collective-permute-start | bytes 392 | tf_op jit(solution)/shard_map/ppermute | solution.py:16
  19.8 24.1 %collective-permute-start.4 = (f32[2,2,1,1024]{3,2,0,1:T(1,128)}, f32[2,2,1,1024]{3,2,0,1:T(1,128)}, u32[]{:S(2)}, u32[]{:S(2)}) collective-permute-start(f32[2,2,1,1024]{3,2,0,1:T(1,128)} %get-tuple-element.20), channel_id=1, source_target_pairs={{0,8},{8,16},{16,24},{24,32},{32,40},{40,48},{48,56},{56,64},{64,7... | collective-permute-start | bytes 49160 | tf_op jit(solution)/shard_map/ppermute | solution.py:24
  30.6 43.6 %collective-permute-start.8 = (f32[2,128,1024]{2,1,0:T(8,128)}, f32[2,128,1024]{2,1,0:T(8,128)}, u32[]{:S(2)}, u32[]{:S(2)}) collective-permute-start(f32[2,128,1024]{2,1,0:T(8,128)} %get-tuple-element.16), channel_id=1, source_target_pairs={{0,128},{1,129},{2,130},{3,131},{4,132},{5,133},{6,134},{7,135},{8... | collective-permute-start | bytes 3145736 | tf_op jit(solution)/shard_map/ppermute | solution.py:16
  31.9 42.3 %collective-permute-start.9 = (f32[2,128,1024]{2,1,0:T(8,128)}, f32[2,128,1024]{2,1,0:T(8,128)}, u32[]{:S(2)}, u32[]{:S(2)}) collective-permute-start(f32[2,128,1024]{2,1,0:T(8,128)} %get-tuple-element.17), channel_id=1, source_target_pairs={{128,0},{129,1},{130,2},{131,3},{132,4},{133,5},{134,6},{135,7},{1... | collective-permute-start | bytes 3145736 | tf_op jit(solution)/shard_map/ppermute | solution.py:16
  38.8 24.7 %collective-permute-start.5 = (f32[2,2,1,1024]{3,2,0,1:T(1,128)}, f32[2,2,1,1024]{3,2,0,1:T(1,128)}, u32[]{:S(2)}, u32[]{:S(2)}) collective-permute-start(f32[2,2,1,1024]{3,2,0,1:T(1,128)} %get-tuple-element.19), channel_id=1, source_target_pairs={{8,0},{16,8},{24,16},{32,24},{40,32},{48,40},{56,48},{64,56},{72,6... | collective-permute-start | bytes 49160 | tf_op jit(solution)/shard_map/ppermute | solution.py:27
  42.9 25.8 %copy-start.2 = (f32[2,2,128,1024]{3,2,0,1:T(8,128)S(1)}, f32[2,2,128,1024]{3,2,0,1:T(8,128)}, u32[]{:S(2)}) copy-start(f32[2,2,128,1024]{3,2,0,1:T(8,128)} %copy-done.1) | copy-start | bytes 6291460
  43.0 25.8 %copy-start.12 = (f32[2,2,8,1024]{3,2,0,1:T(8,128)S(1)}, f32[2,2,8,1024]{3,2,0,1:T(8,128)}, u32[]{:S(2)}) copy-start(f32[2,2,8,1024]{3,2,0,1:T(8,128)} %fusion.34) | copy-start | bytes 393220
  64.4 9.3 %collective-permute-start.6 = (f32[2,2,130,1]{3,2,0,1:T(8,128)S(1)}, f32[2,2,130,1]{3,2,0,1:T(8,128)S(1)}, u32[]{:S(2)}, u32[]{:S(2)}) collective-permute-start(f32[2,2,130,1]{3,2,0,1:T(8,128)S(1)} %get-tuple-element.7), channel_id=1, source_target_pairs={{1,0},{2,1},{3,2},{4,3},{5,4},{6,5},{7,6},{9,8},{10,9},{11,10},{12... | collective-permute-start | bytes 6248 | tf_op jit(solution)/shard_map/ppermute | solution.py:27
  66.3 7.9 %collective-permute-start.7 = (f32[2,2,130,1]{3,2,0,1:T(8,128)S(1)}, f32[2,2,130,1]{3,2,0,1:T(8,128)S(1)}, u32[]{:S(2)}, u32[]{:S(2)}) collective-permute-start(f32[2,2,130,1]{3,2,0,1:T(8,128)S(1)} %get-tuple-element.8), channel_id=1, source_target_pairs={{0,1},{1,2},{2,3},{3,4},{4,5},{5,6},{6,7},{8,9},{9,10},{10,11},{11... | collective-permute-start | bytes 6248 | tf_op jit(solution)/shard_map/ppermute | solution.py:24
  73.3 10.6 %copy-start.8 = (f32[2,2,128,1024]{3,2,0,1:T(8,128)}, f32[2,2,128,1024]{3,2,0,1:T(8,128)S(1)}, u32[]{:S(2)}) copy-start(f32[2,2,128,1024]{3,2,0,1:T(8,128)S(1)} %get-tuple-element.21) | copy-start | bytes 6291460
  77.1 6.8 %copy-start.7 = (f32[2,2,128,1024]{3,2,1,0:T(8,128)S(1)}, f32[2,2,128,1024]{3,2,1,0:T(8,128)}, u32[]{:S(2)}) copy-start(f32[2,2,128,1024]{3,2,1,0:T(8,128)} %param.11) | copy-start | bytes 6291460
  77.1 6.8 %copy-start.20 = (f32[2]{0:T(128)S(1)}, f32[2]{0:T(128)}, u32[]{:S(2)}) copy-start(f32[2]{0:T(128)} %constant.69.clone) | copy-start | bytes 28
  87.8 40.9 %collective-permute-start.14 = (f32[2,128,1024]{2,1,0:T(8,128)S(1)}, f32[2,128,1024]{2,1,0:T(8,128)}, u32[]{:S(2)}, u32[]{:S(2)}) collective-permute-start(f32[2,128,1024]{2,1,0:T(8,128)S(1)} %get-tuple-element.12), channel_id=1, source_target_pairs={{0,128},{1,129},{2,130},{3,131},{4,132},{5,133},{6,134},{7,135},{8... | collective-permute-start | bytes 3145736 | tf_op jit(solution)/shard_map/ppermute | solution.py:16
  89.1 39.6 %collective-permute-start.15 = (f32[2,128,1024]{2,1,0:T(8,128)S(1)}, f32[2,128,1024]{2,1,0:T(8,128)}, u32[]{:S(2)}, u32[]{:S(2)}) collective-permute-start(f32[2,128,1024]{2,1,0:T(8,128)S(1)} %get-tuple-element.13), channel_id=1, source_target_pairs={{128,0},{129,1},{130,2},{131,3},{132,4},{133,5},{134,6},{135,7},{1... | collective-permute-start | bytes 3145736 | tf_op jit(solution)/shard_map/ppermute | solution.py:16
  95.7 5.9 %collective-permute-start.10 = (f32[2,2,1,1024]{3,2,0,1:T(1,128)S(1)}, f32[2,2,1,1024]{3,2,0,1:T(1,128)S(1)}, u32[]{:S(2)}, u32[]{:S(2)}) collective-permute-start(f32[2,2,1,1024]{3,2,0,1:T(1,128)S(1)} %get-tuple-element.10), channel_id=1, source_target_pairs={{0,8},{8,16},{16,24},{24,32},{32,40},{40,48},{48,56},{56,64},{64,7... | collective-permute-start | bytes 49160 | tf_op jit(solution)/shard_map/ppermute | solution.py:24
  97.7 20.9 %collective-permute-start.11 = (f32[2,2,1,1024]{3,2,0,1:T(1,128)S(1)}, f32[2,2,1,1024]{3,2,0,1:T(1,128)S(1)}, u32[]{:S(2)}, u32[]{:S(2)}) collective-permute-start(f32[2,2,1,1024]{3,2,0,1:T(1,128)S(1)} %get-tuple-element.9), channel_id=1, source_target_pairs={{8,0},{16,8},{24,16},{32,24},{40,32},{48,40},{56,48},{64,56},{72,6... | collective-permute-start | bytes 49160 | tf_op jit(solution)/shard_map/ppermute | solution.py:27
  118.7 6.2 %collective-permute-start.12 = (f32[2,2,130,1]{3,2,0,1:T(8,128)S(1)}, f32[2,2,130,1]{3,2,0,1:T(8,128)S(1)}, u32[]{:S(2)}, u32[]{:S(2)}) collective-permute-start(f32[2,2,130,1]{3,2,0,1:T(8,128)S(1)} %get-tuple-element.5), channel_id=1, source_target_pairs={{1,0},{2,1},{3,2},{4,3},{5,4},{6,5},{7,6},{9,8},{10,9},{11,10},{12... | collective-permute-start | bytes 6248 | tf_op jit(solution)/shard_map/ppermute | solution.py:27
  120.9 7.9 %collective-permute-start.13 = (f32[2,2,130,1]{3,2,0,1:T(8,128)S(1)}, f32[2,2,130,1]{3,2,0,1:T(8,128)S(1)}, u32[]{:S(2)}, u32[]{:S(2)}) collective-permute-start(f32[2,2,130,1]{3,2,0,1:T(8,128)S(1)} %get-tuple-element.6), channel_id=1, source_target_pairs={{0,1},{1,2},{2,3},{3,4},{4,5},{5,6},{6,7},{8,9},{9,10},{10,11},{11... | collective-permute-start | bytes 6248 | tf_op jit(solution)/shard_map/ppermute | solution.py:24
  (16 other events, 41.8 us)
where the time goes:
time: 139 us
  starting transfers between devices  47.6 us (34%)
  waiting for transfers between devices  42.8 us (31%)
  other arithmetic  28.8 us (21%)
  local copies, waits for them, and re-layouts  16.3 us (12%)
  matrix products  2.49 us (2%)
    ppermute x4, waiting for transfers between devices, with_halo(): lax.ppermute(lax.slice_in_dim(block, 0, width, axis=dim), axis, backward)  38.5 us
    ppermute x8, starting transfers between devices, shifted(): return lax.ppermute(block, axis, route)  27.2 us
    add x2, other arithmetic, local(): volts = volts + weight_now * (rhs - applied) / diagonal  10.5 us
    ppermute x4, starting transfers between devices, with_halo(): lax.ppermute(lax.slice_in_dim(block, 0, width, axis=dim), axis, backward)  10.5 us
    ppermute x4, starting transfers between devices, with_halo(): lax.ppermute(lax.slice_in_dim(block, block.shape[dim] - width, None, axis...  9.86 us
    unnamed x50, local copies, waits for them, and re-layouts  8.52 us
    sub x1, other arithmetic, local(): applied = diagonal * volts - beside - vertical  6.74 us
    mul x2, other arithmetic, local(): ground * supply * via_down  4.53 us
  transfers between devices with their start and end apart: 16, of which 5 were waited for; matrix products, arithmetic and copies ran while one was open for 14% of the time, Pallas kernels for 0%

commit v1 on v0

v1 whole, which is shorter than its diff:
```python
import jax
import jax.numpy as jnp
from jax import lax
from jax.experimental import pallas as pl
from jax.experimental.pallas import tpu as pltpu
from jax.sharding import PartitionSpec as P

BS = 16
LANES = 128
PAD = 8
W1, W2 = 0.85, 1.35
ALPHA = 1.0 + W2 * (1.0 - W1) / W1
MESH = pl.DeviceIdType.MESH
f32 = jnp.float32


def kernel(
    u_hbm, k_hbm, e_hbm, s_hbm, sites, vias, pat_hbm, pc_hbm, out,
    us, es, ss, ks, xs, ds, ts,
    pat, pc, tab,
    snd_e, snd_w, col_w, col_e, snd_e2, snd_w2, col_w2, col_e2,
    die_snd, die_rcv, die_snd2, die_rcv2,
    load_sem, small_sem, send_sem, recv_sem,
):
    nets, layers, tiles, _, _ = es.shape
    rows = es.shape[3]
    octets = rows // 8
    block_rows = rows // BS
    die, row, col = lax.axis_index("die"), lax.axis_index("row"), lax.axis_index("col")
    n_row, n_col = lax.axis_size("row"), lax.axis_size("col")
    has_n, has_s = row > 0, row < n_row - 1
    has_w, has_e = col > 0, col < n_col - 1
    inner, cross = die, 1 - die

    small = [
        pltpu.make_async_copy(pat_hbm, pat, small_sem.at[0]),
        pltpu.make_async_copy(pc_hbm, pc, small_sem.at[1]),
    ]
    for copy in small:
        copy.start()
    planes = ((u_hbm, us, PAD), (e_hbm, es, 0), (s_hbm, ss, PAD), (k_hbm, ks, 0))
    for a, (src, dst, pad) in enumerate(planes):
        for c in range(tiles):
            pltpu.make_async_copy(
                src.at[:, :, :, c * LANES : (c + 1) * LANES],
                dst.at[:, :, c, pad : pad + rows, :],
                load_sem.at[a],
            ).start()

    def wait_load(a):
        _, dst, pad = planes[a]
        whole = dst.at[:, :, :, pad : pad + rows, :]
        pltpu.make_async_copy(whole, whole, load_sem.at[a]).wait()

    barrier = pltpu.get_barrier_semaphore()

    def greet(there, **where):
        @pl.when(there)
        def _():
            pl.semaphore_signal(barrier, inc=1, device_id=where, device_id_type=MESH)

    greet(has_n, row=row - 1)
    greet(has_s, row=row + 1)
    greet(has_w, col=col - 1)
    greet(has_e, col=col + 1)
    pl.semaphore_signal(barrier, inc=1, device_id={"die": 1 - die}, device_id_type=MESH)

    def message(i, src, dst, **where):
        return pltpu.make_async_remote_copy(
            src_ref=src,
            dst_ref=dst,
            send_sem=send_sem.at[i],
            recv_sem=recv_sem.at[i],
            device_id=where,
            device_id_type=MESH,
        )

    def last_row(ref):
        return ref.at[:, :, :, PAD + rows - 1 : PAD + rows, :]

    def first_row(ref):
        return ref.at[:, :, :, PAD : PAD + 1, :]

    def above(ref):
        return ref.at[:, :, :, PAD - 1 : PAD, :]

    def below(ref):
        return ref.at[:, :, :, PAD + rows : PAD + rows + 1, :]

    south_u = message(0, last_row(us), above(us), row=row + 1)
    south_s = message(1, last_row(ss), above(ss), row=row + 1)
    north_u = message(2, first_row(us), below(us), row=row - 1)
    east_1 = message(3, snd_e, col_w, col=col + 1)
    west_1 = message(4, snd_w, col_e, col=col - 1)
    die_1 = message(5, die_snd, die_rcv, die=1 - die)
    south_d = message(6, last_row(ds), above(ds), row=row + 1)
    north_d = message(7, first_row(ds), below(ds), row=row - 1)
    east_2 = message(8, snd_e2, col_w2, col=col + 1)
    west_2 = message(9, snd_w2, col_e2, col=col - 1)
    die_2 = message(10, die_snd2, die_rcv2, die=1 - die)

    def on(condition, *actions):
        @pl.when(condition)
        def _():
            for action in actions:
                action()

    zero_row = jnp.zeros((tiles, LANES), f32)

    def clear(side, refs, at):
        @pl.when(jnp.logical_not(side))
        def _():
            for ref in refs:
                for n in range(nets):
                    for l in range(layers):
                        ref[n, l, :, at, :] = zero_row

    clear(has_n, (us, ss, ds), PAD - 1)
    clear(has_s, (us, ds), PAD + rows)

    @pl.when(jnp.logical_not(has_w))
    def _():
        col_w[...] = jnp.zeros(col_w.shape, f32)
        col_w2[...] = jnp.zeros(col_w2.shape, f32)

    @pl.when(jnp.logical_not(has_e))
    def _():
        col_e[...] = jnp.zeros(col_e.shape, f32)
        col_e2[...] = jnp.zeros(col_e2.shape, f32)

    lane = lax.broadcasted_iota(jnp.int32, (8, LANES), 1)
    sub = lax.broadcasted_iota(jnp.int32, (8, LANES), 0)
    low = lane % BS
    group = lane // BS

    block_id = jnp.where(low < tiles, sub * (tiles * 8) + low * 8 + group, -1)
    down = [[jnp.zeros((8, LANES), f32) for _ in range(layers)] for _ in range(nets)]
    for l in range(layers):
        for i in range(sites.shape[-1]):
            here = block_id == sites[l, 0, 0, i]
            for n in range(nets):
                down[n][l] = jnp.where(here, vias[n, l, 0, 0, i], down[n][l])

    for copy in small:
        copy.wait()
    across = sub * BS + low
    halves = pc.shape[0] // 8
    for h in range(2):
        for half in range(halves):
            table = jnp.zeros((8, LANES), f32)
            for i in range(8):
                line = jnp.broadcast_to(
                    pc[half * 8 + i : half * 8 + i + 1, h * LANES : (h + 1) * LANES], (8, LANES)
                )
                table = jnp.where(group == i, jnp.take_along_axis(line, across, axis=1), table)
            tab[h, half] = table

    def currents(step, _):
        l, c = step // tiles, step % tiles
        wide = jnp.concatenate([pat[l], pat[l]], axis=1)
        number = jnp.take_along_axis(wide, c * 8 + group, axis=1) * BS + low
        tables = [[tab[h, half] for half in range(halves)] for h in range(2)]
        for b in range(block_rows):
            pick = jnp.broadcast_to(number[b : b + 1, :], (8, LANES))
            within = pick & (LANES - 1)
            upper = pick >= LANES
            for h in range(2):
                value = jnp.where(
                    upper,
                    jnp.take_along_axis(tables[h][1], within, axis=1),
                    jnp.take_along_axis(tables[h][0], within, axis=1),
                )
                at = b * BS + h * 8
                xs[0, l, c, at : at + 8, :] = -value
                xs[1, l, c, at : at + 8, :] = value
        return 0

    lax.fori_loop(0, layers * tiles, currents, 0)

    def centres(pad):
        return pl.ds(pad + BS // 2, block_rows, stride=BS)

    def gather_centres(ref, n, l):
        found = jnp.zeros((8, LANES), f32)
        for c in range(tiles):
            line = pltpu.roll(ref[n, l, c, centres(PAD), :], (c - BS // 2) % LANES, 1)
            found = jnp.where(low == c, line, found)
        return found

    def spread(packed, c):
        return jnp.where(low == BS // 2, pltpu.roll(packed, (BS // 2 - c) % LANES, 1), 0.0)

    def add_centres(ref, n, l, packed, pad, scale=None):
        for c in range(tiles):
            term = spread(packed, c)
            if scale is not None:
                term = term * scale[n, l, c, centres(0), :]
            ref[n, l, c, centres(pad), :] = ref[n, l, c, centres(pad), :] + term

    wait_load(0)
    held = [[gather_centres(us, n, l) for l in range(layers)] for n in range(nets)]
    first_die = die == 0
    for n in range(nets):
        die_snd[n] = jnp.where(first_die, held[n][1], held[n][0])
        die_snd[nets + n] = down[n][0]

    wait_load(1)

    @pl.when(jnp.logical_not(has_e))
    def _():
        for n in range(nets):
            for l in range(layers):
                def edge(o, _, n=n, l=l):
                    at = pl.ds(pl.multiple_of(o * 8, 8), 8)
                    es[n, l, tiles - 1, at, :] = jnp.where(
                        lane == LANES - 1, 0.0, es[n, l, tiles - 1, at, :]
                    )
                    return 0
                lax.fori_loop(0, octets, edge, 0)

    def pack_columns(ref, pad, send_e, send_w, with_e):
        def body(o, _):
            at = pl.multiple_of(o * 8, 8)
            to_e = jnp.zeros((8, LANES), f32)
            to_w = jnp.zeros((8, LANES), f32)
            for n in range(nets):
                for l in range(layers):
                    p = n * layers + l
                    last = ref[n, l, tiles - 1, pl.ds(at + pad, 8), :]
                    to_e = jnp.where(lane == p, pltpu.roll(last, p + 1, 1), to_e)
                    first = ref[n, l, 0, pl.ds(at + pad, 8), :]
                    to_w = jnp.where(lane == p, pltpu.roll(first, p, 1) if p else first, to_w)
                    if with_e:
                        q = nets * layers + p
                        edge = es[n, l, tiles - 1, pl.ds(at, 8), :]
                        to_e = jnp.where(lane == q, pltpu.roll(edge, q + 1, 1), to_e)
            send_e[pl.ds(at, 8), :] = to_e
            send_w[pl.ds(at, 8), :] = to_w
            return 0

        lax.fori_loop(0, octets, body, 0)

    pack_columns(us, PAD, snd_e, snd_w, True)

    wait_load(2)

    @pl.when(jnp.logical_not(has_s))
    def _():
        for n in range(nets):
            for l in range(layers):
                ss[n, l, :, PAD + rows - 1, :] = zero_row

    neighbours = 1 + sum(jnp.where(there, 1, 0) for there in (has_n, has_s, has_w, has_e))
    pl.semaphore_wait(barrier, neighbours)
    on(has_s, south_u.start, south_s.start)
    on(has_n, north_u.start)
    on(has_e, east_1.start)
    on(has_w, west_1.start)
    die_1.start()

    wait_load(3)
    for n in range(nets):
        link = down[n][1]
        package = jnp.where(first_die, down[n][0], 0.0)
        supply = 1.0 if n == 0 else 0.0
        flow = link * (held[n][1] - held[n][0])
        add_centres(ks, n, 0, link + package, 0)
        add_centres(xs, n, 0, flow + package * (supply - held[n][0]), 0)
        add_centres(ks, n, 1, link, 0)
        add_centres(xs, n, 1, -flow, 0)

    def at_lane(v, p, target):
        return pltpu.roll(v, lax.rem(target - p + LANES, LANES), 1)

    def east_of(values, c, halo):
        after = values[c + 1] if c + 1 in values else halo
        return jnp.where(lane == LANES - 1, after, values[c])

    def west_of(values, c, halo):
        before = values[c - 1] if c - 1 in values else halo
        return jnp.where(lane == 0, before, values[c])

    def span(cs, rows_at, reads):
        return [c for c in range(cs[0] - 1, cs[-1] + 2) if 0 <= c < tiles]

    def sweep_1(n, l, at, cs, halos=None, stride=None):
        def ds_(pad):
            return pl.ds(at + pad, 8) if stride is None else pl.ds(at + pad, 8, stride=stride)

        p = n * layers + l
        near = [c for c in range(cs[0] - 1, cs[-1] + 2) if 0 <= c < tiles]
        left = [c for c in near if c <= cs[-1]]
        u = {c: us[n, l, c, ds_(PAD), :] for c in near}
        e = {c: es[n, l, c, ds_(0), :] for c in left}
        turned = {c: pltpu.roll(u[c], LANES - 1, 1) for c in near}
        u_e = e_w = f_w = None
        if halos and tiles - 1 in cs:
            u_e = at_lane(col_e[ds_(0), :], p, LANES - 1)
        if halos and 0 in cs:
            e_w = at_lane(col_w[ds_(0), :], nets * layers + p, 0)
            f_w = e_w * (u[0] - at_lane(col_w[ds_(0), :], p, 0))
        flow = {}
        for c in left:
            if c + 1 in turned:
                flow[c] = e[c] * (east_of(turned, c, None) - u[c])
            else:
                flow[c] = e[c] * (east_of(turned, c, turned[c] if u_e is None else u_e) - u[c])
        flow_t = {c: pltpu.roll(flow[c], 1, 1) for c in left}
        e_t = {c: pltpu.roll(e[c], 1, 1) for c in left}
        for c in cs:
            s = ss[n, l, c, ds_(PAD), :]
            s_n = ss[n, l, c, ds_(PAD - 1), :]
            u_s = us[n, l, c, ds_(PAD + 1), :]
            u_n = us[n, l, c, ds_(PAD - 1), :]
            east_w = west_of(e_t, c, e_t[c] if e_w is None else e_w)
            flow_w = west_of(flow_t, c, flow_t[c] if f_w is None else f_w)
            diagonal = ks[n, l, c, ds_(0), :] + e[c] + east_w + s + s_n
            residual = (
                xs[n, l, c, ds_(0), :] + (flow[c] - flow_w) + (s * (u_s - u[c]) - s_n * (u[c] - u_n))
            )
            inverse = 1.0 / diagonal
            ds[n, l, c, ds_(PAD), :] = residual * (inverse * W1)
            ts[n, l, c, ds_(0), :] = inverse * W2

    def sweep_2(n, l, at, cs, halos):
        p = n * layers + l
        near = [c for c in range(cs[0] - 1, cs[-1] + 2) if 0 <= c < tiles]
        left = [c for c in near if c <= cs[-1]]
        d = {c: ds[n, l, c, pl.ds(at + PAD, 8), :] for c in near}
        e = {c: es[n, l, c, pl.ds(at, 8), :] for c in left}
        turned = {c: pltpu.roll(d[c], LANES - 1, 1) for c in near}
        d_e = g_w = None
        if halos and tiles - 1 in cs:
            d_e = at_lane(col_e2[pl.ds(at, 8), :], p, LANES - 1)
        if halos and 0 in cs:
            e_w = at_lane(col_w[pl.ds(at, 8), :], nets * layers + p, 0)
            g_w = e_w * at_lane(col_w2[pl.ds(at, 8), :], p, 0)
        pull_t = {c: pltpu.roll(e[c] * d[c], 1, 1) for c in left}
        for c in cs:
            s = ss[n, l, c, pl.ds(at + PAD, 8), :]
            s_n = ss[n, l, c, pl.ds(at + PAD - 1, 8), :]
            d_s = ds[n, l, c, pl.ds(at + PAD + 1, 8), :]
            d_n = ds[n, l, c, pl.ds(at + PAD - 1, 8), :]
            beside = (e[c] * east_of(turned, c, d_e) + west_of(pull_t, c, g_w)) + (s * d_s + s_n * d_n)
            out[n, l, pl.ds(at, 8), c * LANES : (c + 1) * LANES] = (
                us[n, l, c, pl.ds(at + PAD, 8), :] + ALPHA * d[c]
            ) + ts[n, l, c, pl.ds(at, 8), :] * beside

    middle = tuple(range(1, tiles - 1))
    every = tuple(range(tiles))
    inside = octets - 2

    def for_inside(sweep, layer, *strips, halos):
        def body(i, _):
            n, o = i // inside, 1 + i % inside
            for cs in strips:
                sweep(n, layer, pl.multiple_of(o * 8, 8), cs, halos)
            return 0

        lax.fori_loop(0, nets * inside, body, 0)

    def for_ends(sweep):
        def body(i, _):
            n, l = i // layers, i % layers
            for o in (0, octets - 1):
                sweep(n, l, o * 8, every, True)
            return 0

        lax.fori_loop(0, nets * layers, body, 0)

    for_inside(sweep_1, inner, middle, halos=False)

    die_1.wait_recv()
    across_die = [jnp.where(first_die, die_rcv[nets + n], down[n][0]) for n in range(nets)]
    for n in range(nets):
        mine = jnp.where(first_die, held[n][1], held[n][0])
        add_centres(ks, n, cross, across_die[n], 0)
        add_centres(xs, n, cross, across_die[n] * (die_rcv[n] - mine), 0)
    for n in range(nets):
        sweep_1(n, cross, BS // 2, every, stride=BS)
    moved_cross = [gather_centres(ds, n, cross) for n in range(nets)]
    for n in range(nets):
        die_snd2[n] = moved_cross[n]

    for_inside(sweep_1, cross, middle, halos=False)
    die_2.start()

    on(has_w, east_1.wait_recv)
    on(has_e, west_1.wait_recv)
    for l in range(layers):
        for_inside(sweep_1, l, (0,), (tiles - 1,), halos=True)

    on(has_n, south_u.wait_recv, south_s.wait_recv)
    on(has_s, north_u.wait_recv)
    for_ends(sweep_1)

    pack_columns(ds, PAD, snd_e2, snd_w2, False)
    on(has_s, south_d.start)
    on(has_n, north_d.start)
    on(has_e, east_2.start)
    on(has_w, west_2.start)

    moved_inner = [gather_centres(ds, n, inner) for n in range(nets)]
    for n in range(nets):
        link = down[n][1]
        add_centres(us, n, cross, link * moved_inner[n], PAD, ts)
        add_centres(us, n, inner, link * moved_cross[n], PAD, ts)
    die_2.wait_recv()
    for n in range(nets):
        add_centres(us, n, cross, across_die[n] * die_rcv2[n], PAD, ts)

    for l in range(layers):
        for_inside(sweep_2, l, middle, halos=False)
    on(has_w, east_2.wait_recv)
    on(has_e, west_2.wait_recv)
    for l in range(layers):
        for_inside(sweep_2, l, (0,), (tiles - 1,), halos=True)
    on(has_n, south_d.wait_recv)
    on(has_s, north_d.wait_recv)
    for_ends(sweep_2)

    on(has_s, south_u.wait_send, south_s.wait_send, south_d.wait_send)
    on(has_n, north_u.wait_send, north_d.wait_send)
    on(has_e, east_1.wait_send, east_2.wait_send)
    on(has_w, west_1.wait_send, west_2.wait_send)
    die_1.wait_send()
    die_2.wait_send()


def local(u, k, e, s, sites, vias, patterns, pattern_currents):
    nets, layers, rows, cols = u.shape
    tiles = cols // LANES
    grid = (nets, layers, tiles, rows, LANES)
    padded = (nets, layers, tiles, rows + 2 * PAD, LANES)
    vmem = pltpu.VMEM
    hbm = pl.BlockSpec(memory_space=pltpu.HBM)
    smem = pl.BlockSpec(memory_space=pltpu.SMEM)
    column = vmem((rows, LANES), f32)
    packed = vmem((nets, 8, LANES), f32)
    return pl.pallas_call(
        kernel,
        out_shape=vmem(u.shape, f32),
        in_specs=[hbm, hbm, hbm, hbm, smem, smem, hbm, hbm],
        out_specs=pl.BlockSpec(memory_space=vmem),
        scratch_shapes=[
            vmem(padded, f32), vmem(grid, f32), vmem(padded, f32), vmem(grid, f32),
            vmem(grid, f32), vmem(padded, f32), vmem(grid, f32),
            vmem(patterns.shape, jnp.int32), vmem(pattern_currents.shape, f32), vmem((2, 2, 8, LANES), f32),
            column, column, column, column, column, column, column, column,
            vmem((2 * nets, 8, LANES), f32), vmem((2 * nets, 8, LANES), f32), packed, packed,
            pltpu.SemaphoreType.DMA((4,)), pltpu.SemaphoreType.DMA((2,)),
            pltpu.SemaphoreType.DMA((11,)), pltpu.SemaphoreType.DMA((11,)),
        ],
        compiler_params=pltpu.CompilerParams(
            collective_id=0, has_side_effects=True, vmem_limit_bytes=64800000
        ),
    )(u, k, e, s, sites, vias, patterns, pattern_currents)


def solution(mesh):
    spec = P(None, "die", "row", "col")
    in_specs = (
        spec,
        spec,
        spec,
        spec,
        P("die", "row", "col", None),
        P(None, "die", "row", "col", None),
        P("die", "row", "col"),
        P(),
    )
    return jax.shard_map(local, mesh=mesh, in_specs=in_specs, out_specs=spec, check_vma=False)
```

time: 139 us -> 40 us (0.29)
  the two profiles are of different devices: /device:TPU:110 before, /device:TPU:71 now
where the time goes in v1:
time: 40 us; the launch traced here: 39.5 us
  Pallas kernels  38.1 us (95%)
  local copies, waits for them, and re-layouts  1.32 us (3%)
    pallas_call x1, Pallas kernels, local(): pl.pallas_call(kernel, out_shape=vmem(u.shape, f32), in_specs=[hbm, hbm,...  38.1 us
    unnamed x1, local copies, waits for them, and re-layouts  1.32 us

profile of v1, /device:TPU:71, one launch (start us, length us, event | category | flops | bytes accessed | tf_op | source)
XLA Modules:
  0.0 39.5 jit_solution(6821714627701657158)
XLA Ops:
  0.0 38.1 %shard_map.82 = f32[2,2,128,1024]{3,2,1,0:T(8,128)S(1)} custom-call(f32[2,2,128,1024]{3,2,1,0:T(8,128)} %u_hbm.1, f32[2,2,128,1024]{3,2,1,0:T(8,128)} %k_hbm.1, f32[2,2,128,1024]{3,2,1,0:T(8,128)} %e_hbm.1, f32[2,2,128,1024]{3,2,1,0:T(8,128)} %s_hbm.1, s32[2,1,1,32]{3,2,1,0:T(1,128)} %sites.1, f32[2,2,1,1,32]{4,3,2,1,0:T(1,128)} %vias.1, ...), custom_call_target="tpu_custom_call" | custom-call | tf_op jit(solution)/shard_map/pallas_call | solution.py:440
  38.1 1.3 %copy.10 = f32[2,2,128,1024]{3,2,1,0:T(8,128)} copy(f32[2,2,128,1024]{3,2,1,0:T(8,128)S(1)} %shard_map.82) | data formatting | bytes 4194304

commit v2 on v1

--- a/solution.py
+++ b/solution.py
@@ -11,12 +11,14 @@
 W1, W2 = 0.85, 1.35
 ALPHA = 1.0 + W2 * (1.0 - W1) / W1
 MESH = pl.DeviceIdType.MESH
+EACH_1, EACH_1C, EACH_2, EACH_2C = 7, 7, 7, 7
+TILES_STEP, PACK_STEP = 4, 4
 f32 = jnp.float32
 
 
 def kernel(
     u_hbm, k_hbm, e_hbm, s_hbm, sites, vias, pat_hbm, pc_hbm, out,
-    us, es, ss, ks, xs, ds, ts,
+    us, es, ss, ks, xs, ds, ts, ws,
     pat, pc, tab,
     snd_e, snd_w, col_w, col_e, snd_e2, snd_w2, col_w2, col_e2,
     die_snd, die_rcv, die_snd2, die_rcv2,
@@ -32,6 +34,19 @@
     has_w, has_e = col > 0, col < n_col - 1
     inner, cross = die, 1 - die
 
+    barrier = pltpu.get_barrier_semaphore()
+
+    def greet(there, **where):
+        @pl.when(there)
+        def _():
+            pl.semaphore_signal(barrier, inc=1, device_id=where, device_id_type=MESH)
+
+    greet(has_n, row=row - 1)
+    greet(has_s, row=row + 1)
+    greet(has_w, col=col - 1)
+    greet(has_e, col=col + 1)
+    pl.semaphore_signal(barrier, inc=1, device_id={"die": 1 - die}, device_id_type=MESH)
+
     small = [
         pltpu.make_async_copy(pat_hbm, pat, small_sem.at[0]),
         pltpu.make_async_copy(pc_hbm, pc, small_sem.at[1]),
@@ -52,19 +67,6 @@
         whole = dst.at[:, :, :, pad : pad + rows, :]
         pltpu.make_async_copy(whole, whole, load_sem.at[a]).wait()
 
-    barrier = pltpu.get_barrier_semaphore()
-
-    def greet(there, **where):
-        @pl.when(there)
-        def _():
-            pl.semaphore_signal(barrier, inc=1, device_id=where, device_id_type=MESH)
-
-    greet(has_n, row=row - 1)
-    greet(has_s, row=row + 1)
-    greet(has_w, col=col - 1)
-    greet(has_e, col=col + 1)
-    pl.semaphore_signal(barrier, inc=1, device_id={"die": 1 - die}, device_id_type=MESH)
-
     def message(i, src, dst, **where):
         return pltpu.make_async_remote_copy(
             src_ref=src,
@@ -156,26 +158,29 @@
             tab[h, half] = table
 
     def currents(step, _):
-        l, c = step // tiles, step % tiles
+        l = lax.div(step, tiles // TILES_STEP)
+        base = lax.rem(step, tiles // TILES_STEP) * TILES_STEP
         wide = jnp.concatenate([pat[l], pat[l]], axis=1)
-        number = jnp.take_along_axis(wide, c * 8 + group, axis=1) * BS + low
         tables = [[tab[h, half] for half in range(halves)] for h in range(2)]
-        for b in range(block_rows):
-            pick = jnp.broadcast_to(number[b : b + 1, :], (8, LANES))
-            within = pick & (LANES - 1)
-            upper = pick >= LANES
-            for h in range(2):
-                value = jnp.where(
-                    upper,
-                    jnp.take_along_axis(tables[h][1], within, axis=1),
-                    jnp.take_along_axis(tables[h][0], within, axis=1),
-                )
-                at = b * BS + h * 8
-                xs[0, l, c, at : at + 8, :] = -value
-                xs[1, l, c, at : at + 8, :] = value
+        for k in range(TILES_STEP):
+            c = base + k
+            number = jnp.take_along_axis(wide, c * 8 + group, axis=1) * BS + low
+            for b in range(block_rows):
+                pick = jnp.broadcast_to(number[b : b + 1, :], (8, LANES))
+                within = pick & (LANES - 1)
+                upper = pick >= LANES
+                for h in range(2):
+                    value = jnp.where(
+                        upper,
+                        jnp.take_along_axis(tables[h][1], within, axis=1),
+                        jnp.take_along_axis(tables[h][0], within, axis=1),
+                    )
+                    at = b * BS + h * 8
+                    xs[0, l, c, at : at + 8, :] = -value
+                    xs[1, l, c, at : at + 8, :] = value
         return 0
 
-    lax.fori_loop(0, layers * tiles, currents, 0)
+    lax.fori_loop(0, layers * tiles // TILES_STEP, currents, 0)
 
     def centres(pad):
         return pl.ds(pad + BS // 2, block_rows, stride=BS)
@@ -190,12 +195,16 @@
     def spread(packed, c):
         return jnp.where(low == BS // 2, pltpu.roll(packed, (BS // 2 - c) % LANES, 1), 0.0)
 
-    def add_centres(ref, n, l, packed, pad, scale=None):
-        for c in range(tiles):
-            term = spread(packed, c)
-            if scale is not None:
-                term = term * scale[n, l, c, centres(0), :]
-            ref[n, l, c, centres(pad), :] = ref[n, l, c, centres(pad), :] + term
+    def add_centres(updates, pad):
+        fresh = []
+        for ref, n, l, packed, scale in updates:
+            for c in range(tiles):
+                term = spread(packed, c)
+                if scale is not None:
+                    term = term * scale[n, l, c, centres(0), :]
+                fresh.append((ref, n, l, c, ref[n, l, c, centres(pad), :] + term))
+        for ref, n, l, c, value in fresh:
+            ref[n, l, c, centres(pad), :] = value
 
     wait_load(0)
     held = [[gather_centres(us, n, l) for l in range(layers)] for n in range(nets)]
@@ -219,8 +228,12 @@
                 lax.fori_loop(0, octets, edge, 0)
 
     def pack_columns(ref, pad, send_e, send_w, with_e):
-        def body(o, _):
-            at = pl.multiple_of(o * 8, 8)
+        def body(step, _):
+            for k in range(PACK_STEP):
+                pack(pl.multiple_of(step * (8 * PACK_STEP) + k * 8, 8))
+            return 0
+
+        def pack(at):
             to_e = jnp.zeros((8, LANES), f32)
             to_w = jnp.zeros((8, LANES), f32)
             for n in range(nets):
@@ -236,9 +249,8 @@
                         to_e = jnp.where(lane == q, pltpu.roll(edge, q + 1, 1), to_e)
             send_e[pl.ds(at, 8), :] = to_e
             send_w[pl.ds(at, 8), :] = to_w
-            return 0
-
-        lax.fori_loop(0, octets, body, 0)
+
+        lax.fori_loop(0, octets // PACK_STEP, body, 0)
 
     pack_columns(us, PAD, snd_e, snd_w, True)
 
@@ -264,24 +276,24 @@
         package = jnp.where(first_die, down[n][0], 0.0)
         supply = 1.0 if n == 0 else 0.0
         flow = link * (held[n][1] - held[n][0])
-        add_centres(ks, n, 0, link + package, 0)
-        add_centres(xs, n, 0, flow + package * (supply - held[n][0]), 0)
-        add_centres(ks, n, 1, link, 0)
-        add_centres(xs, n, 1, -flow, 0)
+        add_centres(
+            [
+                (ks, n, 0, link + package, None),
+                (xs, n, 0, flow + package * (supply - held[n][0]), None),
+                (ks, n, 1, link, None),
+                (xs, n, 1, -flow, None),
+            ],
+            0,
+        )
 
     def at_lane(v, p, target):
         return pltpu.roll(v, lax.rem(target - p + LANES, LANES), 1)
 
-    def east_of(values, c, halo):
-        after = values[c + 1] if c + 1 in values else halo
-        return jnp.where(lane == LANES - 1, after, values[c])
-
-    def west_of(values, c, halo):
-        before = values[c - 1] if c - 1 in values else halo
-        return jnp.where(lane == 0, before, values[c])
-
-    def span(cs, rows_at, reads):
-        return [c for c in range(cs[0] - 1, cs[-1] + 2) if 0 <= c < tiles]
+    def from_east(turned, c):
+        return jnp.where(lane == LANES - 1, turned.get(c + 1, turned[c]), turned[c])
+
+    def from_west(turned, c):
+        return jnp.where(lane == 0, turned.get(c - 1, turned[c]), turned[c])
 
     def sweep_1(n, l, at, cs, halos=None, stride=None):
         def ds_(pad):
@@ -290,105 +302,108 @@
         p = n * layers + l
         near = [c for c in range(cs[0] - 1, cs[-1] + 2) if 0 <= c < tiles]
         left = [c for c in near if c <= cs[-1]]
+        right = [c for c in near if c >= cs[0]]
         u = {c: us[n, l, c, ds_(PAD), :] for c in near}
         e = {c: es[n, l, c, ds_(0), :] for c in left}
-        turned = {c: pltpu.roll(u[c], LANES - 1, 1) for c in near}
-        u_e = e_w = f_w = None
+        u_e = {c: pltpu.roll(u[c], LANES - 1, 1) for c in right}
+        u_w = {c: pltpu.roll(u[c], 1, 1) for c in left}
+        e_w = {c: pltpu.roll(e[c], 1, 1) for c in left}
         if halos and tiles - 1 in cs:
-            u_e = at_lane(col_e[ds_(0), :], p, LANES - 1)
+            u_e[tiles] = at_lane(col_e[ds_(0), :], p, LANES - 1)
         if halos and 0 in cs:
-            e_w = at_lane(col_w[ds_(0), :], nets * layers + p, 0)
-            f_w = e_w * (u[0] - at_lane(col_w[ds_(0), :], p, 0))
-        flow = {}
-        for c in left:
-            if c + 1 in turned:
-                flow[c] = e[c] * (east_of(turned, c, None) - u[c])
-            else:
-                flow[c] = e[c] * (east_of(turned, c, turned[c] if u_e is None else u_e) - u[c])
-        flow_t = {c: pltpu.roll(flow[c], 1, 1) for c in left}
-        e_t = {c: pltpu.roll(e[c], 1, 1) for c in left}
+            u_w[-1] = at_lane(col_w[ds_(0), :], p, 0)
+            e_w[-1] = at_lane(col_w[ds_(0), :], nets * layers + p, 0)
         for c in cs:
             s = ss[n, l, c, ds_(PAD), :]
             s_n = ss[n, l, c, ds_(PAD - 1), :]
             u_s = us[n, l, c, ds_(PAD + 1), :]
             u_n = us[n, l, c, ds_(PAD - 1), :]
-            east_w = west_of(e_t, c, e_t[c] if e_w is None else e_w)
-            flow_w = west_of(flow_t, c, flow_t[c] if f_w is None else f_w)
-            diagonal = ks[n, l, c, ds_(0), :] + e[c] + east_w + s + s_n
+            west = from_west(e_w, c)
+            diagonal = (ks[n, l, c, ds_(0), :] + e[c]) + (west + s) + s_n
             residual = (
-                xs[n, l, c, ds_(0), :] + (flow[c] - flow_w) + (s * (u_s - u[c]) - s_n * (u[c] - u_n))
+                xs[n, l, c, ds_(0), :]
+                + (e[c] * (from_east(u_e, c) - u[c]) - west * (u[c] - from_west(u_w, c)))
+                + (s * (u_s - u[c]) - s_n * (u[c] - u_n))
             )
             inverse = 1.0 / diagonal
             ds[n, l, c, ds_(PAD), :] = residual * (inverse * W1)
             ts[n, l, c, ds_(0), :] = inverse * W2
+            ws[n, l, c, ds_(0), :] = west
 
     def sweep_2(n, l, at, cs, halos):
         p = n * layers + l
+        here, mid = pl.ds(at, 8), pl.ds(at + PAD, 8)
         near = [c for c in range(cs[0] - 1, cs[-1] + 2) if 0 <= c < tiles]
-        left = [c for c in near if c <= cs[-1]]
-        d = {c: ds[n, l, c, pl.ds(at + PAD, 8), :] for c in near}
-        e = {c: es[n, l, c, pl.ds(at, 8), :] for c in left}
-        turned = {c: pltpu.roll(d[c], LANES - 1, 1) for c in near}
-        d_e = g_w = None
+        d = {c: ds[n, l, c, mid, :] for c in near}
+        d_e = {c: pltpu.roll(d[c], LANES - 1, 1) for c in near if c >= cs[0]}
+        d_w = {c: pltpu.roll(d[c], 1, 1) for c in near if c <= cs[-1]}
         if halos and tiles - 1 in cs:
-            d_e = at_lane(col_e2[pl.ds(at, 8), :], p, LANES - 1)
+            d_e[tiles] = at_lane(col_e2[here, :], p, LANES - 1)
         if halos and 0 in cs:
-            e_w = at_lane(col_w[pl.ds(at, 8), :], nets * layers + p, 0)
-            g_w = e_w * at_lane(col_w2[pl.ds(at, 8), :], p, 0)
-        pull_t = {c: pltpu.roll(e[c] * d[c], 1, 1) for c in left}
+            d_w[-1] = at_lane(col_w2[here, :], p, 0)
         for c in cs:
-            s = ss[n, l, c, pl.ds(at + PAD, 8), :]
-            s_n = ss[n, l, c, pl.ds(at + PAD - 1, 8), :]
-            d_s = ds[n, l, c, pl.ds(at + PAD + 1, 8), :]
-            d_n = ds[n, l, c, pl.ds(at + PAD - 1, 8), :]
-            beside = (e[c] * east_of(turned, c, d_e) + west_of(pull_t, c, g_w)) + (s * d_s + s_n * d_n)
-            out[n, l, pl.ds(at, 8), c * LANES : (c + 1) * LANES] = (
-                us[n, l, c, pl.ds(at + PAD, 8), :] + ALPHA * d[c]
-            ) + ts[n, l, c, pl.ds(at, 8), :] * beside
+            beside = (
+                es[n, l, c, here, :] * from_east(d_e, c) + ws[n, l, c, here, :] * from_west(d_w, c)
+            ) + (
+                ss[n, l, c, mid, :] * ds[n, l, c, pl.ds(at + PAD + 1, 8), :]
+                + ss[n, l, c, pl.ds(at + PAD - 1, 8), :] * ds[n, l, c, pl.ds(at + PAD - 1, 8), :]
+            )
+            out[n, l, here, c * LANES : (c + 1) * LANES] = (
+                us[n, l, c, mid, :] + ALPHA * d[c]
+            ) + ts[n, l, c, here, :] * beside
 
     middle = tuple(range(1, tiles - 1))
     every = tuple(range(tiles))
     inside = octets - 2
 
-    def for_inside(sweep, layer, *strips, halos):
+    def for_inside(sweep, layer, *strips, halos, each):
+        groups = inside // each
+
         def body(i, _):
-            n, o = i // inside, 1 + i % inside
-            for cs in strips:
-                sweep(n, layer, pl.multiple_of(o * 8, 8), cs, halos)
+            n = lax.div(i, groups)
+            base = 1 + lax.rem(i, groups) * each
+            for k in range(each):
+                for cs in strips:
+                    sweep(n, layer, pl.multiple_of((base + k) * 8, 8), cs, halos)
             return 0
 
-        lax.fori_loop(0, nets * inside, body, 0)
+        lax.fori_loop(0, nets * groups, body, 0)
 
     def for_ends(sweep):
         def body(i, _):
-            n, l = i // layers, i % layers
+            n, l = lax.div(i, layers), lax.rem(i, layers)
             for o in (0, octets - 1):
                 sweep(n, l, o * 8, every, True)
             return 0
 
         lax.fori_loop(0, nets * layers, body, 0)
 
-    for_inside(sweep_1, inner, middle, halos=False)
+    for_inside(sweep_1, inner, middle, halos=False, each=EACH_1)
 
     die_1.wait_recv()
     across_die = [jnp.where(first_die, die_rcv[nets + n], down[n][0]) for n in range(nets)]
     for n in range(nets):
         mine = jnp.where(first_die, held[n][1], held[n][0])
-        add_centres(ks, n, cross, across_die[n], 0)
-        add_centres(xs, n, cross, across_die[n] * (die_rcv[n] - mine), 0)
+        add_centres(
+            [
+                (ks, n, cross, across_die[n], None),
+                (xs, n, cross, across_die[n] * (die_rcv[n] - mine), None),
+            ],
+            0,
+        )
     for n in range(nets):
         sweep_1(n, cross, BS // 2, every, stride=BS)
     moved_cross = [gather_centres(ds, n, cross) for n in range(nets)]
     for n in range(nets):
         die_snd2[n] = moved_cross[n]
 
-    for_inside(sweep_1, cross, middle, halos=False)
+    for_inside(sweep_1, cross, middle, halos=False, each=EACH_1)
     die_2.start()
 
     on(has_w, east_1.wait_recv)
     on(has_e, west_1.wait_recv)
     for l in range(layers):
-        for_inside(sweep_1, l, (0,), (tiles - 1,), halos=True)
+        for_inside(sweep_1, l, (0,), (tiles - 1,), halos=True, each=EACH_1C)
 
     on(has_n, south_u.wait_recv, south_s.wait_recv)
     on(has_s, north_u.wait_recv)
@@ -400,21 +415,21 @@
     on(has_e, east_2.start)
     on(has_w, west_2.start)
 
+    die_2.wait_recv()
     moved_inner = [gather_centres(ds, n, inner) for n in range(nets)]
     for n in range(nets):
         link = down[n][1]
-        add_centres(us, n, cross, link * moved_inner[n], PAD, ts)
-        add_centres(us, n, inner, link * moved_cross[n], PAD, ts)
-    die_2.wait_recv()
-    for n in range(nets):
-        add_centres(us, n, cross, across_die[n] * die_rcv2[n], PAD, ts)
+        moved = link * moved_inner[n] + across_die[n] * die_rcv2[n]
+        add_centres(
+            [(us, n, cross, moved, ts), (us, n, inner, link * moved_cross[n], ts)], PAD
+        )
 
     for l in range(layers):
-        for_inside(sweep_2, l, middle, halos=False)
+        for_inside(sweep_2, l, middle, halos=False, each=EACH_2)
     on(has_w, east_2.wait_recv)
     on(has_e, west_2.wait_recv)
     for l in range(layers):
-        for_inside(sweep_2, l, (0,), (tiles - 1,), halos=True)
+        for_inside(sweep_2, l, (0,), (tiles - 1,), halos=True, each=EACH_2C)
     on(has_n, south_d.wait_recv)
     on(has_s, north_d.wait_recv)
     for_ends(sweep_2)
@@ -444,7 +459,7 @@
         out_specs=pl.BlockSpec(memory_space=vmem),
         scratch_shapes=[
             vmem(padded, f32), vmem(grid, f32), vmem(padded, f32), vmem(grid, f32),
-            vmem(grid, f32), vmem(padded, f32), vmem(grid, f32),
+            vmem(grid, f32), vmem(padded, f32), vmem(grid, f32), vmem(grid, f32),
             vmem(patterns.shape, jnp.int32), vmem(pattern_currents.shape, f32), vmem((2, 2, 8, LANES), f32),
             column, column, column, column, column, column, column, column,
             vmem((2 * nets, 8, LANES), f32), vmem((2 * nets, 8, LANES), f32), packed, packed,

time: 40 us -> 19.2 us (0.48)
  the two profiles are of different devices: /device:TPU:71 before, /device:TPU:1 now
where the time goes in v2:
time: 19.2 us; the launch traced here: 19 us
  Pallas kernels  17.7 us (92%)
  local copies, waits for them, and re-layouts  1.32 us (7%)
    pallas_call x1, Pallas kernels, local(): pl.pallas_call(kernel, out_shape=vmem(u.shape, f32), in_specs=[hbm, hbm,...  17.7 us
    unnamed x1, local copies, waits for them, and re-layouts  1.32 us

profile of v2, /device:TPU:1, one launch (start us, length us, event | category | flops | bytes accessed | tf_op | source)
XLA Modules:
  0.0 19.0 jit_solution(14693901762282804444)
XLA Ops:
  0.0 17.7 %shard_map.82 = f32[2,2,128,1024]{3,2,1,0:T(8,128)S(1)} custom-call(f32[2,2,128,1024]{3,2,1,0:T(8,128)} %u_hbm.1, f32[2,2,128,1024]{3,2,1,0:T(8,128)} %k_hbm.1, f32[2,2,128,1024]{3,2,1,0:T(8,128)} %e_hbm.1, f32[2,2,128,1024]{3,2,1,0:T(8,128)} %s_hbm.1, s32[2,1,1,32]{3,2,1,0:T(1,128)} %sites.1, f32[2,2,1,1,32]{4,3,2,1,0:T(1,128)} %vias.1, ...), custom_call_target="tpu_custom_call" | custom-call | tf_op jit(solution)/shard_map/pallas_call | solution.py:455
  17.7 1.3 %copy.10 = f32[2,2,128,1024]{3,2,1,0:T(8,128)} copy(f32[2,2,128,1024]{3,2,1,0:T(8,128)S(1)} %shard_map.82) | data formatting | bytes 4194304

commit v3 on v0

v3 whole, which is shorter than its diff:
```python
import jax
import jax.numpy as jnp
from jax import lax
from jax.experimental import pallas as pl
from jax.experimental.pallas import tpu as pltpu
from jax.sharding import PartitionSpec as P

BS = 16
LANES = 128
VMEM_LIMIT = 64800000
PAD = 8
W1, W2 = 0.85, 1.35
ALPHA = W1 + W2 * (1.0 - W1)
BETA = W1 * W2
MESH = pl.DeviceIdType.MESH
EACH_1, EACH_2 = 8, 8
TILES_STEP, PACK_STEP, FIX_STEP = 2, 4, 4
N_U, N_S, S_U, N_D, S_D = range(5)
f32 = jnp.float32


def kernel(
    u_hbm, k_hbm, e_hbm, s_hbm, site_hbm, via_hbm, pat_hbm, pc_hbm, out,
    us, es, ss, ks, xs, ds, ts, ws, halo,
    sites, vias, pat, pc, tab,
    snd_e, snd_w, col_w, col_e, snd_e2, snd_w2, col_w2, col_e2,
    die_snd, die_rcv, die_snd2, die_rcv2,
    load_sem, small_sem, send_sem, recv_sem,
):
    nets, layers, tiles, rows, _ = es.shape
    octets = rows // 8
    block_rows = rows // BS
    planes = [(n, l) for n in range(nets) for l in range(layers)]
    die, row, col = lax.axis_index("die"), lax.axis_index("row"), lax.axis_index("col")
    n_row, n_col = lax.axis_size("row"), lax.axis_size("col")
    has_n, has_s = row > 0, row < n_row - 1
    has_w, has_e = col > 0, col < n_col - 1
    first_die = die == 0

    barrier = pltpu.get_barrier_semaphore()

    def greet(there, **where):
        @pl.when(there)
        def _():
            pl.semaphore_signal(barrier, inc=1, device_id=where, device_id_type=MESH)

    greet(has_n, row=row - 1)
    greet(has_s, row=row + 1)
    greet(has_w, col=col - 1)
    greet(has_e, col=col + 1)
    pl.semaphore_signal(barrier, inc=1, device_id={"die": 1 - die}, device_id_type=MESH)

    def load(src, dst, pad, c, sem):
        pltpu.make_async_copy(
            src.at[:, :, :, c * LANES : (c + 1) * LANES], dst.at[:, :, c, pad : pad + rows, :], sem
        ).start()

    def loaded(whole, sem):
        pltpu.make_async_copy(whole, whole, sem).wait()

    for c in range(tiles):
        load(u_hbm, us, PAD, c, load_sem.at[0])
    load(e_hbm, es, 0, tiles - 1, load_sem.at[1])
    for c in range(tiles):
        load(s_hbm, ss, PAD, c, load_sem.at[2])
    small = [
        pltpu.make_async_copy(src, dst, small_sem.at[i])
        for i, (src, dst) in enumerate(((site_hbm, sites), (via_hbm, vias), (pat_hbm, pat), (pc_hbm, pc)))
    ]
    for copy in small:
        copy.start()
    for c in range(tiles - 1):
        load(e_hbm, es, 0, c, load_sem.at[3])
    for c in range(tiles):
        load(k_hbm, ks, 0, c, load_sem.at[4])

    last = PAD + rows - 1
    zero_row = jnp.zeros((tiles, LANES), f32)
    for n, l in planes:
        for ref, at in ((us, PAD - 1), (us, PAD + rows), (ss, PAD - 1), (ds, PAD - 1), (ds, PAD + rows)):
            ref[n, l, :, at, :] = zero_row

    def message(i, src, dst, **where):
        return pltpu.make_async_remote_copy(
            src_ref=src,
            dst_ref=dst,
            send_sem=send_sem.at[i],
            recv_sem=recv_sem.at[i],
            device_id=where,
            device_id_type=MESH,
        )

    def line(ref, at):
        return ref.at[:, :, :, at : at + 1, :]

    south_u = message(0, line(us, last), line(halo, N_U), row=row + 1)
    south_s = message(1, line(ss, last), line(halo, N_S), row=row + 1)
    north_u = message(2, line(us, PAD), line(halo, S_U), row=row - 1)
    east_1 = message(3, snd_e, col_w, col=col + 1)
    west_1 = message(4, snd_w, col_e, col=col - 1)
    die_1 = message(5, die_snd, die_rcv, die=1 - die)
    south_d = message(6, line(ds, last), line(halo, N_D), row=row + 1)
    north_d = message(7, line(ds, PAD), line(halo, S_D), row=row - 1)
    east_2 = message(8, snd_e2, col_w2, col=col + 1)
    west_2 = message(9, snd_w2, col_e2, col=col - 1)
    die_2 = message(10, die_snd2, die_rcv2, die=1 - die)

    def on(condition, *actions):
        @pl.when(condition)
        def _():
            for action in actions:
                action()

    def clear(side, *at):
        @pl.when(jnp.logical_not(side))
        def _():
            for n, l in planes:
                for i in at:
                    halo[n, l, :, i, :] = zero_row

    clear(has_n, N_U, N_S, N_D)
    clear(has_s, S_U, S_D)

    def clear_columns(side, *refs):
        @pl.when(jnp.logical_not(side))
        def _():
            for ref in refs:
                ref[...] = jnp.zeros(ref.shape, f32)

    clear_columns(has_w, col_w, col_w2)
    clear_columns(has_e, col_e, col_e2)

    lane = lax.broadcasted_iota(jnp.int32, (8, LANES), 1)
    sub = lax.broadcasted_iota(jnp.int32, (8, LANES), 0)
    low = lane % BS
    group = lane // BS

    loaded(us.at[:, :, :, PAD : PAD + rows, :], load_sem.at[0])
    loaded(es.at[:, :, tiles - 1], load_sem.at[1])

    @pl.when(jnp.logical_not(has_e))
    def _():
        for n, l in planes:
            for o in range(octets):
                at = slice(o * 8, o * 8 + 8)
                es[n, l, tiles - 1, at, :] = jnp.where(lane == LANES - 1, 0.0, es[n, l, tiles - 1, at, :])

    def pack_columns():
        def body(step, _):
            for k in range(PACK_STEP):
                pack(pl.multiple_of(step * (8 * PACK_STEP) + k * 8, 8))
            return 0

        def pack(at):
            to_e = jnp.zeros((8, LANES), f32)
            to_w = jnp.zeros((8, LANES), f32)
            for p, (n, l) in enumerate(planes):
                final = us[n, l, tiles - 1, pl.ds(at + PAD, 8), :]
                to_e = jnp.where(lane == p, pltpu.roll(final, p + 1, 1), to_e)
                first = us[n, l, 0, pl.ds(at + PAD, 8), :]
                to_w = jnp.where(lane == p, pltpu.roll(first, p, 1) if p else first, to_w)
                q = len(planes) + p
                edge = es[n, l, tiles - 1, pl.ds(at, 8), :]
                to_e = jnp.where(lane == q, pltpu.roll(edge, q + 1, 1), to_e)
            snd_e[pl.ds(at, 8), :] = to_e
            snd_w[pl.ds(at, 8), :] = to_w

        lax.fori_loop(0, octets // PACK_STEP, body, 0)

    pack_columns()

    loaded(ss.at[:, :, :, PAD : PAD + rows, :], load_sem.at[2])

    @pl.when(jnp.logical_not(has_s))
    def _():
        for n, l in planes:
            ss[n, l, :, last, :] = zero_row

    neighbours = 1 + sum(jnp.where(there, 1, 0) for there in (has_n, has_s, has_w, has_e))
    pl.semaphore_wait(barrier, neighbours)
    on(has_s, south_u.start, south_s.start)
    on(has_n, north_u.start)
    on(has_e, east_1.start)
    on(has_w, west_1.start)

    for copy in small[:2]:
        copy.wait()
    block_id = jnp.where(low < tiles, sub * (tiles * 8) + low * 8 + group, -1)
    down = [[jnp.zeros((8, LANES), f32) for _ in range(layers)] for _ in range(nets)]
    for l in range(layers):
        for i in range(sites.shape[-1]):
            here = block_id == sites[l, 0, 0, i]
            for n in range(nets):
                down[n][l] = jnp.where(here, vias[n, l, 0, 0, i], down[n][l])

    def centres(pad):
        return pl.ds(pad + BS // 2, block_rows, stride=BS)

    def gather_centres(ref, n, l):
        found = jnp.zeros((8, LANES), f32)
        for c in range(tiles):
            cells = pltpu.roll(ref[n, l, c, centres(PAD), :], (c - BS // 2) % LANES, 1)
            found = jnp.where(low == c, cells, found)
        return found

    def spread(packed, c):
        return jnp.where(low == BS // 2, pltpu.roll(packed, (BS // 2 - c) % LANES, 1), 0.0)

    held = [[gather_centres(us, n, l) for l in range(layers)] for n in range(nets)]
    for n in range(nets):
        die_snd[n] = jnp.where(first_die, held[n][1], held[n][0])
        die_snd[nets + n] = down[n][0]

    die_1.start()

    for copy in small[2:]:
        copy.wait()
    across = sub * BS + low
    patterns = pc.shape[0]

    for i in range(patterns):
        for h in range(2):
            part = jnp.broadcast_to(pc[i : i + 1, h * LANES : (h + 1) * LANES], (8, LANES))
            tab[h, i] = jnp.take_along_axis(part, across, axis=1)

    def currents(step, _):
        per = tiles // TILES_STEP
        l = lax.div(step, per)
        base = lax.rem(step, per) * TILES_STEP
        wide = jnp.concatenate([pat[l], pat[l]], axis=1)
        tables = [[tab[h, i] for i in range(patterns)] for h in range(2)]
        for k in range(TILES_STEP):
            c = base + k
            number = jnp.take_along_axis(wide, c * 8 + group, axis=1)
            for b in range(block_rows):
                mine = jnp.broadcast_to(number[b : b + 1, :], (8, LANES))
                bits = []
                bit = 1
                while bit < patterns:
                    bits.append((mine & bit) != 0)
                    bit *= 2
                for h in range(2):
                    values = tables[h]
                    for odd in bits:
                        values = [
                            jnp.where(odd, values[i + 1], values[i]) for i in range(0, len(values), 2)
                        ]
                    at = b * BS + h * 8
                    xs[l, c, at : at + 8, :] = values[0]
        return 0

    lax.fori_loop(0, layers * tiles // TILES_STEP, currents, 0)

    loaded(es.at[:, :, : tiles - 1], load_sem.at[3])
    loaded(ks, load_sem.at[4])


    def sweep_1(n, l, at):
        here, mid, up, dn = (pl.ds(at + i, 8) for i in (0, PAD, PAD - 1, PAD + 1))

        def fetch(c):
            u, e = us[n, l, c, mid, :], es[n, l, c, here, :]
            return u, e, pltpu.roll(u, LANES - 1, 1), pltpu.roll(u, 1, 1), pltpu.roll(e, 1, 1)

        before, now = (0.0,) * 5, fetch(0)
        for c in range(tiles):
            after = fetch(c + 1) if c + 1 < tiles else (0.0,) * 5
            u, e, u_e, u_w, e_w = now
            u_e = jnp.where(lane == LANES - 1, after[2], u_e)
            u_w = jnp.where(lane == 0, before[3], u_w)
            west = jnp.where(lane == 0, before[4], e_w)
            k, s, s_n = ks[n, l, c, here, :], ss[n, l, c, mid, :], ss[n, l, c, up, :]
            x = xs[l, c, here, :]
            diagonal = (k + e) + (west + s) + s_n
            beside = (e * u_e + west * u_w) + (s * us[n, l, c, dn, :] + s_n * us[n, l, c, up, :])
            rest = k * u + (x if n else -x)
            inverse = 1.0 / diagonal
            ds[n, l, c, mid, :] = (rest + beside) * inverse - u
            ts[n, l, c, here, :] = inverse * BETA
            ws[n, l, c, here, :] = west
            before, now = now, after

    def sweep_2(n, l, at):
        here, mid, up, dn = (pl.ds(at + i, 8) for i in (0, PAD, PAD - 1, PAD + 1))

        def fetch(c):
            d = ds[n, l, c, mid, :]
            return d, pltpu.roll(d, LANES - 1, 1), pltpu.roll(d, 1, 1)

        before, now = (0.0,) * 3, fetch(0)
        for c in range(tiles):
            after = fetch(c + 1) if c + 1 < tiles else (0.0,) * 3
            d, d_e, d_w = now
            d_e = jnp.where(lane == LANES - 1, after[1], d_e)
            d_w = jnp.where(lane == 0, before[2], d_w)
            beside = (es[n, l, c, here, :] * d_e + ws[n, l, c, here, :] * d_w) + (
                ss[n, l, c, mid, :] * ds[n, l, c, dn, :] + ss[n, l, c, up, :] * ds[n, l, c, up, :]
            )
            out[n, l, c, here, :] = (us[n, l, c, mid, :] + ALPHA * d) + ts[n, l, c, here, :] * beside
            before, now = now, after

    def everywhere(sweep, n, each):
        groups = octets // each

        def body(i, _):
            l = lax.div(i, groups)
            base = lax.rem(i, groups) * each
            for k in range(each):
                sweep(n, l, pl.multiple_of((base + k) * 8, 8))
            return 0

        lax.fori_loop(0, layers * groups, body, 0)

    for n in range(nets):
        everywhere(sweep_1, n, EACH_1)

    def turn(v, source, target):
        shift = (target - source) % LANES
        return pltpu.roll(v, shift, 1) if shift else v

    def in_columns(fix):
        def body(step, _):
            for k in range(FIX_STEP):
                at = pl.multiple_of(step * (8 * FIX_STEP) + k * 8, 8)
                for p, (n, l) in enumerate(planes):
                    fix(p, n, l, at)
            return 0

        lax.fori_loop(0, octets // FIX_STEP, body, 0)

    die_1.wait_recv()
    link = [down[n][1] for n in range(nets)]
    outer = [[down[n][0], jnp.where(first_die, die_rcv[nets + n], 0.0)] for n in range(nets)]
    fresh = []
    for n, l in planes:
        beyond = die_rcv[n]
        if l == 0:
            beyond = jnp.where(first_die, 1.0 if n == 0 else 0.0, beyond)
        total = link[n] + outer[n][l]
        pull = link[n] * (held[n][1 - l] - held[n][l]) + outer[n][l] * (beyond - held[n][l])
        for c in range(tiles):
            t = ts[n, l, c, centres(0), :]
            a = t * (1.0 / BETA)
            scale = 1.0 / (1.0 + a * spread(total, c))
            fresh.append(
                (n, l, c, (ds[n, l, c, centres(PAD), :] + a * spread(pull, c)) * scale, t * scale)
            )
    for n, l, c, d, t in fresh:
        ds[n, l, c, centres(PAD), :] = d
        ts[n, l, c, centres(0), :] = t
    moved = [[gather_centres(ds, n, l) for l in range(layers)] for n in range(nets)]
    for n in range(nets):
        die_snd2[n] = jnp.where(first_die, moved[n][1], moved[n][0])

    on(has_n, south_u.wait_recv, south_s.wait_recv)
    on(has_s, north_u.wait_recv)
    fresh = []
    for n, l in planes:
        t, u = ts[n, l, :, 0, :], us[n, l, :, PAD, :]
        part = t * halo[n, l, :, N_S, :] * (1.0 / BETA)
        scale = 1.0 / (1.0 + part)
        gain = ts[n, l, :, rows - 1, :] * ss[n, l, :, last, :] * (1.0 / BETA)
        fresh.append(
            (
                n,
                l,
                (ds[n, l, :, PAD, :] + part * (halo[n, l, :, N_U, :] - u)) * scale,
                t * scale,
                ds[n, l, :, last, :] + gain * halo[n, l, :, S_U, :],
            )
        )
    for n, l, d, t, d_last in fresh:
        ds[n, l, :, PAD, :] = d
        ts[n, l, :, 0, :] = t
        ds[n, l, :, last, :] = d_last

    die_2.start()
    on(has_w, east_1.wait_recv)
    on(has_e, west_1.wait_recv)

    def join_columns(step, _):
        for k in range(FIX_STEP):
            at = pl.multiple_of(step * (8 * FIX_STEP) + k * 8, 8)
            here, mid = pl.ds(at, 8), pl.ds(at + PAD, 8)
            c = tiles - 1
            to_e = jnp.zeros((8, LANES), f32)
            to_w = jnp.zeros((8, LANES), f32)
            from_e, from_w = col_e[here, :], col_w[here, :]
            fresh = []
            for p, (n, l) in enumerate(planes):
                gain = ts[n, l, c, here, :] * es[n, l, c, here, :] * (1.0 / BETA)
                final = ds[n, l, c, mid, :] + jnp.where(
                    lane == LANES - 1, gain * turn(from_e, p, LANES - 1), 0.0
                )
                t, first, u = ts[n, l, 0, here, :], ds[n, l, 0, mid, :], us[n, l, 0, mid, :]
                edge = turn(from_w, len(planes) + p, 0)
                part = jnp.where(lane == 0, t * edge * (1.0 / BETA), 0.0)
                scale = 1.0 / (1.0 + part)
                first = (first + part * (turn(from_w, p, 0) - u)) * scale
                to_e = jnp.where(lane == p, turn(final, LANES - 1, p), to_e)
                to_w = jnp.where(lane == p, turn(first, 0, p), to_w)
                fresh.append((n, l, final, first, t * scale))
            snd_e2[here, :] = to_e
            snd_w2[here, :] = to_w
            for n, l, final, first, t in fresh:
                ds[n, l, c, mid, :] = final
                ds[n, l, 0, mid, :] = first
                ts[n, l, 0, here, :] = t
        return 0

    lax.fori_loop(0, octets // FIX_STEP, join_columns, 0)

    on(has_s, south_d.start)
    on(has_n, north_d.start)
    on(has_e, east_2.start)
    on(has_w, west_2.start)

    for n in range(nets):
        everywhere(sweep_2, n, EACH_2)

    on(has_w, east_2.wait_recv)
    on(has_e, west_2.wait_recv)

    def join_columns_2(p, n, l, at):
        here = pl.ds(at, 8)
        c = tiles - 1
        gain = ts[n, l, c, here, :] * es[n, l, c, here, :]
        final = out[n, l, c, here, :] + jnp.where(
            lane == LANES - 1, gain * turn(col_e2[here, :], p, LANES - 1), 0.0
        )
        edge = turn(col_w[here, :], len(planes) + p, 0)
        first = out[n, l, 0, here, :] + jnp.where(
            lane == 0, ts[n, l, 0, here, :] * edge * turn(col_w2[here, :], p, 0), 0.0
        )
        out[n, l, c, here, :] = final
        out[n, l, 0, here, :] = first

    in_columns(join_columns_2)

    die_2.wait_recv()
    fresh = []
    for n, l in planes:
        reach = outer[n][l] if l else jnp.where(first_die, 0.0, outer[n][l])
        pull = link[n] * moved[n][1 - l] + reach * die_rcv2[n]
        for c in range(tiles):
            value = out[n, l, c, centres(0), :] + ts[n, l, c, centres(0), :] * spread(pull, c)
            fresh.append((n, l, c, value))
    for n, l, c, value in fresh:
        out[n, l, c, centres(0), :] = value

    on(has_n, south_d.wait_recv)
    on(has_s, north_d.wait_recv)
    fresh = []
    for n, l in planes:
        first = ts[n, l, :, 0, :] * halo[n, l, :, N_S, :] * halo[n, l, :, N_D, :]
        final = ts[n, l, :, rows - 1, :] * ss[n, l, :, last, :] * halo[n, l, :, S_D, :]
        fresh.append((n, l, out[n, l, :, 0, :] + first, out[n, l, :, rows - 1, :] + final))
    for n, l, first, final in fresh:
        out[n, l, :, 0, :] = first
        out[n, l, :, rows - 1, :] = final

    on(has_s, south_u.wait_send, south_s.wait_send, south_d.wait_send)
    on(has_n, north_u.wait_send, north_d.wait_send)
    on(has_e, east_1.wait_send, east_2.wait_send)
    on(has_w, west_1.wait_send, west_2.wait_send)
    die_1.wait_send()
    die_2.wait_send()


def store(cells, out, sem):
    nets, layers, tiles, _, _ = cells.shape
    copies = [
        pltpu.make_async_copy(
            cells.at[n, l, c], out.at[n, l, :, c * LANES : (c + 1) * LANES], sem.at[n, l, c]
        )
        for n in range(nets)
        for l in range(layers)
        for c in range(tiles)
    ]
    for copy in copies:
        copy.start()
    for copy in copies:
        copy.wait()


def local(u, k, e, s, sites, vias, patterns, pattern_currents):
    nets, layers, rows, cols = u.shape
    tiles = cols // LANES
    grid = (nets, layers, tiles, rows, LANES)
    padded = (nets, layers, tiles, rows + 2 * PAD, LANES)
    vmem = pltpu.VMEM
    hbm = pl.BlockSpec(memory_space=pltpu.HBM)
    on_chip = pl.BlockSpec(memory_space=vmem)
    column = vmem((rows, LANES), f32)
    packed = vmem((nets, 8, LANES), f32)
    limit = VMEM_LIMIT
    cells = pl.pallas_call(
        kernel,
        out_shape=vmem(grid, f32),
        in_specs=[hbm] * 8,
        out_specs=on_chip,
        scratch_shapes=[
            vmem(padded, f32), vmem(grid, f32), vmem(padded, f32), vmem(grid, f32),
            vmem(grid[1:], f32), vmem(padded, f32), vmem(grid, f32), vmem(grid, f32),
            vmem((nets, layers, tiles, 8, LANES), f32),
            pltpu.SMEM(sites.shape, jnp.int32), pltpu.SMEM(vias.shape, f32),
            vmem(patterns.shape, jnp.int32), vmem(pattern_currents.shape, f32), vmem((2,) + pattern_currents.shape[:1] + (8, LANES), f32),
            column, column, column, column, column, column, column, column,
            vmem((2 * nets, 8, LANES), f32), vmem((2 * nets, 8, LANES), f32), packed, packed,
            pltpu.SemaphoreType.DMA((5,)), pltpu.SemaphoreType.DMA((4,)),
            pltpu.SemaphoreType.DMA((11,)), pltpu.SemaphoreType.DMA((11,)),
        ],
        compiler_params=pltpu.CompilerParams(
            collective_id=0, has_side_effects=True, vmem_limit_bytes=limit
        ),
    )(u, k, e, s, sites, vias, patterns, pattern_currents)
    return pl.pallas_call(
        store,
        out_shape=jax.ShapeDtypeStruct(u.shape, f32),
        in_specs=[on_chip],
        out_specs=hbm,
        scratch_shapes=[pltpu.SemaphoreType.DMA((nets, layers, tiles))],
        compiler_params=pltpu.CompilerParams(vmem_limit_bytes=1024 * 1024),
    )(cells)


def solution(mesh):
    spec = P(None, "die", "row", "col")
    in_specs = (
        spec,
        spec,
        spec,
        spec,
        P("die", "row", "col", None),
        P(None, "die", "row", "col", None),
        P("die", "row", "col"),
        P(),
    )
    return jax.shard_map(local, mesh=mesh, in_specs=in_specs, out_specs=spec, check_vma=False)
```

time: 139 us -> 17.1 us (0.12)
  the two profiles are of different devices: /device:TPU:110 before, /device:TPU:78 now
where the time goes in v3:
time: 17.1 us; the launch traced here: 17 us
  Pallas kernels  17 us (99%)
    pallas_call x1, Pallas kernels, local(): pl.pallas_call(kernel, out_shape=vmem(grid, f32), in_specs=[hbm] * 8, out...  15.5 us
    pallas_call x1, Pallas kernels, local(): pl.pallas_call(store, out_shape=jax.ShapeDtypeStruct(u.shape, f32), in_sp...  1.57 us

profile of v3, /device:TPU:78, one launch (start us, length us, event | category | flops | bytes accessed | tf_op | source)
XLA Modules:
  0.0 17.0 jit_solution(8616043547583440175)
XLA Ops:
  0.0 15.5 %shard_map.82.cells = f32[2,2,8,128,128]{4,3,2,1,0:T(8,128)S(1)} custom-call(f32[2,2,128,1024]{3,2,1,0:T(8,128)} %u_hbm.1, f32[2,2,128,1024]{3,2,1,0:T(8,128)} %k_hbm.1, f32[2,2,128,1024]{3,2,1,0:T(8,128)} %e_hbm.1, f32[2,2,128,1024]{3,2,1,0:T(8,128)} %s_hbm.1, s32[2,1,1,32]{3,2,1,0:T(1,128)} %site_hbm.1, f32[2,2,1,1,32]{4,3,2,1,0:T(1,128)} %via_hbm.1, ...), custom_call_target="tpu_custom_call" | custom-call | tf_op jit(solution)/shard_map/pallas_call | solution.py:497
  15.5 1.6 %shard_map.83 = f32[2,2,128,1024]{3,2,1,0:T(8,128)} custom-call(f32[2,2,8,128,128]{4,3,2,1,0:T(8,128)S(1)} %shard_map.82.cells), custom_call_target="tpu_custom_call" | custom-call | tf_op jit(solution)/shard_map/pallas_call | solution.py:517

commit v4 on v3

--- a/solution.py
+++ b/solution.py
@@ -13,9 +13,9 @@
 ALPHA = W1 + W2 * (1.0 - W1)
 BETA = W1 * W2
 MESH = pl.DeviceIdType.MESH
-EACH_1, EACH_2 = 8, 8
-TILES_STEP, PACK_STEP, FIX_STEP = 2, 4, 4
-N_U, N_S, S_U, N_D, S_D = range(5)
+EACH_1, EACH_2 = 7, 8
+TILES_STEP, PACK_STEP, FIX_STEP, FIX_INSIDE = 2, 4, 4, 7
+N_U, N_S, S_U, N_D, S_D, N_T, S_T = range(7)
 f32 = jnp.float32
 
 
@@ -23,7 +23,7 @@
     u_hbm, k_hbm, e_hbm, s_hbm, site_hbm, via_hbm, pat_hbm, pc_hbm, out,
     us, es, ss, ks, xs, ds, ts, ws, halo,
     sites, vias, pat, pc, tab,
-    snd_e, snd_w, col_w, col_e, snd_e2, snd_w2, col_w2, col_e2,
+    snd_e, snd_w, col_w, col_e, snd_e2, snd_w2, col_w2, col_e2, thin, thin_rcv,
     die_snd, die_rcv, die_snd2, die_rcv2,
     load_sem, small_sem, send_sem, recv_sem,
 ):
@@ -60,9 +60,9 @@
 
     for c in range(tiles):
         load(u_hbm, us, PAD, c, load_sem.at[0])
-    load(e_hbm, es, 0, tiles - 1, load_sem.at[1])
     for c in range(tiles):
         load(s_hbm, ss, PAD, c, load_sem.at[2])
+    load(e_hbm, es, 0, tiles - 1, load_sem.at[1])
     small = [
         pltpu.make_async_copy(src, dst, small_sem.at[i])
         for i, (src, dst) in enumerate(((site_hbm, sites), (via_hbm, vias), (pat_hbm, pat), (pc_hbm, pc)))
@@ -96,13 +96,15 @@
     south_u = message(0, line(us, last), line(halo, N_U), row=row + 1)
     south_s = message(1, line(ss, last), line(halo, N_S), row=row + 1)
     north_u = message(2, line(us, PAD), line(halo, S_U), row=row - 1)
-    east_1 = message(3, snd_e, col_w, col=col + 1)
-    west_1 = message(4, snd_w, col_e, col=col - 1)
+    east_1 = message(3, thin.at[0], thin_rcv.at[0], col=col + 1)
+    west_1 = message(4, thin.at[1], thin_rcv.at[1], col=col - 1)
     die_1 = message(5, die_snd, die_rcv, die=1 - die)
     south_d = message(6, line(ds, last), line(halo, N_D), row=row + 1)
     north_d = message(7, line(ds, PAD), line(halo, S_D), row=row - 1)
-    east_2 = message(8, snd_e2, col_w2, col=col + 1)
-    west_2 = message(9, snd_w2, col_e2, col=col - 1)
+    east_2 = message(8, thin.at[2], thin_rcv.at[2], col=col + 1)
+    west_2 = message(9, thin.at[3], thin_rcv.at[3], col=col - 1)
+    south_t = message(11, line(ts, rows - 1), line(halo, N_T), row=row + 1)
+    north_t = message(12, line(ts, 0), line(halo, S_T), row=row - 1)
     die_2 = message(10, die_snd2, die_rcv2, die=1 - die)
 
     def on(condition, *actions):
@@ -118,32 +120,50 @@
                 for i in at:
                     halo[n, l, :, i, :] = zero_row
 
-    clear(has_n, N_U, N_S, N_D)
-    clear(has_s, S_U, S_D)
-
-    def clear_columns(side, *refs):
+    clear(has_n, N_U, N_S, N_D, N_T)
+    clear(has_s, S_U, S_D, S_T)
+
+    def clear_columns(side, *slots):
         @pl.when(jnp.logical_not(side))
         def _():
-            for ref in refs:
-                ref[...] = jnp.zeros(ref.shape, f32)
-
-    clear_columns(has_w, col_w, col_w2)
-    clear_columns(has_e, col_e, col_e2)
+            for i in slots:
+                thin_rcv[i] = jnp.zeros(thin_rcv.shape[1:], f32)
+
+    clear_columns(has_w, 0, 2)
+    clear_columns(has_e, 1, 3)
+
+    def make_thin(i, ref):
+        thin[i] = jnp.transpose(ref[...])[: thin.shape[1]]
+
+    def make_wide(i, ref):
+        few = thin_rcv[i]
+        rest = jnp.zeros((LANES - few.shape[0], LANES), f32)
+        ref[...] = jnp.transpose(jnp.concatenate([few, rest], axis=0))
 
     lane = lax.broadcasted_iota(jnp.int32, (8, LANES), 1)
     sub = lax.broadcasted_iota(jnp.int32, (8, LANES), 0)
     low = lane % BS
     group = lane // BS
 
-    loaded(us.at[:, :, :, PAD : PAD + rows, :], load_sem.at[0])
-    loaded(es.at[:, :, tiles - 1], load_sem.at[1])
-
-    @pl.when(jnp.logical_not(has_e))
-    def _():
-        for n, l in planes:
-            for o in range(octets):
-                at = slice(o * 8, o * 8 + 8)
-                es[n, l, tiles - 1, at, :] = jnp.where(lane == LANES - 1, 0.0, es[n, l, tiles - 1, at, :])
+    for copy in small[:2]:
+        copy.wait()
+    block_id = jnp.where(low < tiles, sub * (tiles * 8) + low * 8 + group, -1)
+    down = [[jnp.zeros((8, LANES), f32) for _ in range(layers)] for _ in range(nets)]
+    for l in range(layers):
+        for i in range(sites.shape[-1]):
+            here = block_id == sites[l, 0, 0, i]
+            for n in range(nets):
+                down[n][l] = jnp.where(here, vias[n, l, 0, 0, i], down[n][l])
+
+    for copy in small[2:]:
+        copy.wait()
+    across = sub * BS + low
+    patterns = pc.shape[0]
+
+    for i in range(patterns):
+        for h in range(2):
+            part = jnp.broadcast_to(pc[i : i + 1, h * LANES : (h + 1) * LANES], (8, LANES))
+            tab[h, i] = jnp.take_along_axis(part, across, axis=1)
 
     def pack_columns():
         def body(step, _):
@@ -167,8 +187,7 @@
 
         lax.fori_loop(0, octets // PACK_STEP, body, 0)
 
-    pack_columns()
-
+    loaded(us.at[:, :, :, PAD : PAD + rows, :], load_sem.at[0])
     loaded(ss.at[:, :, :, PAD : PAD + rows, :], load_sem.at[2])
 
     @pl.when(jnp.logical_not(has_s))
@@ -180,18 +199,20 @@
     pl.semaphore_wait(barrier, neighbours)
     on(has_s, south_u.start, south_s.start)
     on(has_n, north_u.start)
+    loaded(es.at[:, :, tiles - 1], load_sem.at[1])
+
+    @pl.when(jnp.logical_not(has_e))
+    def _():
+        for n, l in planes:
+            for o in range(octets):
+                at = slice(o * 8, o * 8 + 8)
+                es[n, l, tiles - 1, at, :] = jnp.where(lane == LANES - 1, 0.0, es[n, l, tiles - 1, at, :])
+
+    pack_columns()
+    make_thin(0, snd_e)
+    make_thin(1, snd_w)
     on(has_e, east_1.start)
     on(has_w, west_1.start)
-
-    for copy in small[:2]:
-        copy.wait()
-    block_id = jnp.where(low < tiles, sub * (tiles * 8) + low * 8 + group, -1)
-    down = [[jnp.zeros((8, LANES), f32) for _ in range(layers)] for _ in range(nets)]
-    for l in range(layers):
-        for i in range(sites.shape[-1]):
-            here = block_id == sites[l, 0, 0, i]
-            for n in range(nets):
-                down[n][l] = jnp.where(here, vias[n, l, 0, 0, i], down[n][l])
 
     def centres(pad):
         return pl.ds(pad + BS // 2, block_rows, stride=BS)
@@ -212,16 +233,6 @@
         die_snd[nets + n] = down[n][0]
 
     die_1.start()
-
-    for copy in small[2:]:
-        copy.wait()
-    across = sub * BS + low
-    patterns = pc.shape[0]
-
-    for i in range(patterns):
-        for h in range(2):
-            part = jnp.broadcast_to(pc[i : i + 1, h * LANES : (h + 1) * LANES], (8, LANES))
-            tab[h, i] = jnp.take_along_axis(part, across, axis=1)
 
     def currents(step, _):
         per = tiles // TILES_STEP
@@ -299,20 +310,26 @@
             out[n, l, c, here, :] = (us[n, l, c, mid, :] + ALPHA * d) + ts[n, l, c, here, :] * beside
             before, now = now, after
 
-    def everywhere(sweep, n, each):
-        groups = octets // each
-
+    def over(sweep, n, first, each, groups):
         def body(i, _):
             l = lax.div(i, groups)
-            base = lax.rem(i, groups) * each
+            base = first + lax.rem(i, groups) * each
             for k in range(each):
                 sweep(n, l, pl.multiple_of((base + k) * 8, 8))
             return 0
 
         lax.fori_loop(0, layers * groups, body, 0)
 
+    def ends(n):
+        def body(l, _):
+            for o in (0, octets - 1):
+                sweep_1(n, l, o * 8)
+            return 0
+
+        lax.fori_loop(0, layers, body, 0)
+
     for n in range(nets):
-        everywhere(sweep_1, n, EACH_1)
+        ends(n)
 
     def turn(v, source, target):
         shift = (target - source) % LANES
@@ -327,6 +344,55 @@
             return 0
 
         lax.fori_loop(0, octets // FIX_STEP, body, 0)
+
+    on(has_w, east_1.wait_recv)
+    on(has_e, west_1.wait_recv)
+    make_wide(0, col_w)
+    make_wide(1, col_e)
+
+    def join_columns(at, send):
+        here, mid = pl.ds(at, 8), pl.ds(at + PAD, 8)
+        c = tiles - 1
+        to_e = jnp.zeros((8, LANES), f32)
+        to_w = jnp.zeros((8, LANES), f32)
+        from_e, from_w = col_e[here, :], col_w[here, :]
+        fresh = []
+        for p, (n, l) in enumerate(planes):
+            gain = ts[n, l, c, here, :] * es[n, l, c, here, :] * (1.0 / BETA)
+            final = ds[n, l, c, mid, :] + jnp.where(
+                lane == LANES - 1, gain * turn(from_e, p, LANES - 1), 0.0
+            )
+            t, first, u = ts[n, l, 0, here, :], ds[n, l, 0, mid, :], us[n, l, 0, mid, :]
+            edge = turn(from_w, len(planes) + p, 0)
+            part = jnp.where(lane == 0, t * edge * (1.0 / BETA), 0.0)
+            scale = 1.0 / (1.0 + part)
+            first = (first + part * (turn(from_w, p, 0) - u)) * scale
+            if send:
+                to_e = jnp.where(lane == p, turn(final, LANES - 1, p), to_e)
+                to_w = jnp.where(lane == p, turn(first, 0, p), to_w)
+            fresh.append((n, l, final, first, t * scale))
+        if send:
+            snd_e2[here, :] = to_e
+            snd_w2[here, :] = to_w
+        for n, l, final, first, t in fresh:
+            ds[n, l, c, mid, :] = final
+            ds[n, l, 0, mid, :] = first
+            ts[n, l, 0, here, :] = t
+
+    for o in (0, octets - 1):
+        join_columns(o * 8, False)
+    on(has_s, south_d.start, south_t.start)
+    on(has_n, north_d.start, north_t.start)
+
+    for n in range(nets):
+        over(sweep_1, n, 1, EACH_1, (octets - 2) // EACH_1)
+
+    def join_inside(step, _):
+        for k in range(FIX_INSIDE):
+            join_columns(pl.multiple_of((1 + step * FIX_INSIDE + k) * 8, 8), True)
+        return 0
+
+    lax.fori_loop(0, (octets - 2) // FIX_INSIDE, join_inside, 0)
 
     die_1.wait_recv()
     link = [down[n][1] for n in range(nets)]
@@ -352,8 +418,12 @@
     for n in range(nets):
         die_snd2[n] = jnp.where(first_die, moved[n][1], moved[n][0])
 
+    die_2.start()
+
     on(has_n, south_u.wait_recv, south_s.wait_recv)
     on(has_s, north_u.wait_recv)
+    on(has_s, south_d.wait_send, south_t.wait_send)
+    on(has_n, north_d.wait_send, north_t.wait_send)
     fresh = []
     for n, l in planes:
         t, u = ts[n, l, :, 0, :], us[n, l, :, PAD, :]
@@ -374,52 +444,27 @@
         ts[n, l, :, 0, :] = t
         ds[n, l, :, last, :] = d_last
 
-    die_2.start()
-    on(has_w, east_1.wait_recv)
-    on(has_e, west_1.wait_recv)
-
-    def join_columns(step, _):
-        for k in range(FIX_STEP):
-            at = pl.multiple_of(step * (8 * FIX_STEP) + k * 8, 8)
-            here, mid = pl.ds(at, 8), pl.ds(at + PAD, 8)
-            c = tiles - 1
-            to_e = jnp.zeros((8, LANES), f32)
-            to_w = jnp.zeros((8, LANES), f32)
-            from_e, from_w = col_e[here, :], col_w[here, :]
-            fresh = []
-            for p, (n, l) in enumerate(planes):
-                gain = ts[n, l, c, here, :] * es[n, l, c, here, :] * (1.0 / BETA)
-                final = ds[n, l, c, mid, :] + jnp.where(
-                    lane == LANES - 1, gain * turn(from_e, p, LANES - 1), 0.0
-                )
-                t, first, u = ts[n, l, 0, here, :], ds[n, l, 0, mid, :], us[n, l, 0, mid, :]
-                edge = turn(from_w, len(planes) + p, 0)
-                part = jnp.where(lane == 0, t * edge * (1.0 / BETA), 0.0)
-                scale = 1.0 / (1.0 + part)
-                first = (first + part * (turn(from_w, p, 0) - u)) * scale
-                to_e = jnp.where(lane == p, turn(final, LANES - 1, p), to_e)
-                to_w = jnp.where(lane == p, turn(first, 0, p), to_w)
-                fresh.append((n, l, final, first, t * scale))
-            snd_e2[here, :] = to_e
-            snd_w2[here, :] = to_w
-            for n, l, final, first, t in fresh:
-                ds[n, l, c, mid, :] = final
-                ds[n, l, 0, mid, :] = first
-                ts[n, l, 0, here, :] = t
-        return 0
-
-    lax.fori_loop(0, octets // FIX_STEP, join_columns, 0)
-
-    on(has_s, south_d.start)
-    on(has_n, north_d.start)
+    for o in (0, octets - 1):
+        here, mid = slice(o * 8, o * 8 + 8), slice(o * 8 + PAD, o * 8 + PAD + 8)
+        to_e = jnp.zeros((8, LANES), f32)
+        to_w = jnp.zeros((8, LANES), f32)
+        for p, (n, l) in enumerate(planes):
+            to_e = jnp.where(lane == p, turn(ds[n, l, tiles - 1, mid, :], LANES - 1, p), to_e)
+            to_w = jnp.where(lane == p, turn(ds[n, l, 0, mid, :], 0, p), to_w)
+        snd_e2[here, :] = to_e
+        snd_w2[here, :] = to_w
+    make_thin(2, snd_e2)
+    make_thin(3, snd_w2)
     on(has_e, east_2.start)
     on(has_w, west_2.start)
 
     for n in range(nets):
-        everywhere(sweep_2, n, EACH_2)
+        over(sweep_2, n, 0, EACH_2, octets // EACH_2)
 
     on(has_w, east_2.wait_recv)
     on(has_e, west_2.wait_recv)
+    make_wide(2, col_w2)
+    make_wide(3, col_e2)
 
     def join_columns_2(p, n, l, at):
         here = pl.ds(at, 8)
@@ -448,19 +493,25 @@
     for n, l, c, value in fresh:
         out[n, l, c, centres(0), :] = value
 
-    on(has_n, south_d.wait_recv)
-    on(has_s, north_d.wait_recv)
+    on(has_n, south_d.wait_recv, south_t.wait_recv)
+    on(has_s, north_d.wait_recv, north_t.wait_recv)
     fresh = []
     for n, l in planes:
-        first = ts[n, l, :, 0, :] * halo[n, l, :, N_S, :] * halo[n, l, :, N_D, :]
-        final = ts[n, l, :, rows - 1, :] * ss[n, l, :, last, :] * halo[n, l, :, S_D, :]
+        north, south = halo[n, l, :, N_S, :], ss[n, l, :, last, :]
+        d_n = halo[n, l, :, N_D, :] + halo[n, l, :, N_T, :] * (1.0 / BETA) * north * us[n, l, :, PAD, :]
+        part = halo[n, l, :, S_T, :] * (1.0 / BETA) * south
+        d_s = (halo[n, l, :, S_D, :] + part * (us[n, l, :, last, :] - halo[n, l, :, S_U, :])) / (
+            1.0 + part
+        )
+        first = ts[n, l, :, 0, :] * north * d_n
+        final = ts[n, l, :, rows - 1, :] * south * d_s
         fresh.append((n, l, out[n, l, :, 0, :] + first, out[n, l, :, rows - 1, :] + final))
     for n, l, first, final in fresh:
         out[n, l, :, 0, :] = first
         out[n, l, :, rows - 1, :] = final
 
-    on(has_s, south_u.wait_send, south_s.wait_send, south_d.wait_send)
-    on(has_n, north_u.wait_send, north_d.wait_send)
+    on(has_s, south_u.wait_send, south_s.wait_send)
+    on(has_n, north_u.wait_send)
     on(has_e, east_1.wait_send, east_2.wait_send)
     on(has_w, west_1.wait_send, west_2.wait_send)
     die_1.wait_send()
@@ -506,9 +557,10 @@
             pltpu.SMEM(sites.shape, jnp.int32), pltpu.SMEM(vias.shape, f32),
             vmem(patterns.shape, jnp.int32), vmem(pattern_currents.shape, f32), vmem((2,) + pattern_currents.shape[:1] + (8, LANES), f32),
             column, column, column, column, column, column, column, column,
+            vmem((4, 16, LANES), f32), vmem((4, 16, LANES), f32),
             vmem((2 * nets, 8, LANES), f32), vmem((2 * nets, 8, LANES), f32), packed, packed,
             pltpu.SemaphoreType.DMA((5,)), pltpu.SemaphoreType.DMA((4,)),
-            pltpu.SemaphoreType.DMA((11,)), pltpu.SemaphoreType.DMA((11,)),
+            pltpu.SemaphoreType.DMA((13,)), pltpu.SemaphoreType.DMA((13,)),
         ],
         compiler_params=pltpu.CompilerParams(
             collective_id=0, has_side_effects=True, vmem_limit_bytes=limit

time: 17.1 us -> 16.8 us (0.982)
  the two profiles are of different devices: /device:TPU:78 before, /device:TPU:71 now
where the time goes in v4:
time: 16.8 us; the launch traced here: 16.7 us
  Pallas kernels  16.7 us (99%)
    pallas_call x1, Pallas kernels, local(): pl.pallas_call(kernel, out_shape=vmem(grid, f32), in_specs=[hbm] * 8, out...  15.1 us
    pallas_call x1, Pallas kernels, local(): pl.pallas_call(store, out_shape=jax.ShapeDtypeStruct(u.shape, f32), in_sp...  1.57 us

profile of v4, /device:TPU:71, one launch (start us, length us, event | category | flops | bytes accessed | tf_op | source)
XLA Modules:
  0.0 16.7 jit_solution(11147221975971971915)
XLA Ops:
  0.0 15.1 %shard_map.82.cells = f32[2,2,8,128,128]{4,3,2,1,0:T(8,128)S(1)} custom-call(f32[2,2,128,1024]{3,2,1,0:T(8,128)} %u_hbm.1, f32[2,2,128,1024]{3,2,1,0:T(8,128)} %k_hbm.1, f32[2,2,128,1024]{3,2,1,0:T(8,128)} %e_hbm.1, f32[2,2,128,1024]{3,2,1,0:T(8,128)} %s_hbm.1, s32[2,1,1,32]{3,2,1,0:T(1,128)} %site_hbm.1, f32[2,2,1,1,32]{4,3,2,1,0:T(1,128)} %via_hbm.1, ...), custom_call_target="tpu_custom_call" | custom-call | tf_op jit(solution)/shard_map/pallas_call | solution.py:548
  15.1 1.6 %shard_map.83 = f32[2,2,128,1024]{3,2,1,0:T(8,128)} custom-call(f32[2,2,8,128,128]{4,3,2,1,0:T(8,128)S(1)} %shard_map.82.cells), custom_call_target="tpu_custom_call" | custom-call | tf_op jit(solution)/shard_map/pallas_call | solution.py:569

commit v5 on v4

--- a/solution.py
+++ b/solution.py
@@ -461,6 +461,17 @@
     for n in range(nets):
         over(sweep_2, n, 0, EACH_2, octets // EACH_2)
 
+    die_2.wait_recv()
+    fresh = []
+    for n, l in planes:
+        reach = outer[n][l] if l else jnp.where(first_die, 0.0, outer[n][l])
+        pull = link[n] * moved[n][1 - l] + reach * die_rcv2[n]
+        for c in range(tiles):
+            value = out[n, l, c, centres(0), :] + ts[n, l, c, centres(0), :] * spread(pull, c)
+            fresh.append((n, l, c, value))
+    for n, l, c, value in fresh:
+        out[n, l, c, centres(0), :] = value
+
     on(has_w, east_2.wait_recv)
     on(has_e, west_2.wait_recv)
     make_wide(2, col_w2)
@@ -481,17 +492,6 @@
         out[n, l, 0, here, :] = first
 
     in_columns(join_columns_2)
-
-    die_2.wait_recv()
-    fresh = []
-    for n, l in planes:
-        reach = outer[n][l] if l else jnp.where(first_die, 0.0, outer[n][l])
-        pull = link[n] * moved[n][1 - l] + reach * die_rcv2[n]
-        for c in range(tiles):
-            value = out[n, l, c, centres(0), :] + ts[n, l, c, centres(0), :] * spread(pull, c)
-            fresh.append((n, l, c, value))
-    for n, l, c, value in fresh:
-        out[n, l, c, centres(0), :] = value
 
     on(has_n, south_d.wait_recv, south_t.wait_recv)
     on(has_s, north_d.wait_recv, north_t.wait_recv)

time: 16.8 us -> 16.6 us (0.988)
  Pallas kernels: 16.7 us -> 16.5 us
where the time goes in v5:
time: 16.6 us; the launch traced here: 16.5 us
  Pallas kernels  16.5 us (99%)
    pallas_call x1, Pallas kernels, local(): pl.pallas_call(kernel, out_shape=vmem(grid, f32), in_specs=[hbm] * 8, out...  14.9 us
    pallas_call x1, Pallas kernels, local(): pl.pallas_call(store, out_shape=jax.ShapeDtypeStruct(u.shape, f32), in_sp...  1.57 us

profile of v5, /device:TPU:71, one launch (start us, length us, event | category | flops | bytes accessed | tf_op | source)
XLA Modules:
  0.0 16.5 jit_solution(14038776114205264140)
XLA Ops:
  0.0 14.9 %shard_map.82.cells = f32[2,2,8,128,128]{4,3,2,1,0:T(8,128)S(1)} custom-call(f32[2,2,128,1024]{3,2,1,0:T(8,128)} %u_hbm.1, f32[2,2,128,1024]{3,2,1,0:T(8,128)} %k_hbm.1, f32[2,2,128,1024]{3,2,1,0:T(8,128)} %e_hbm.1, f32[2,2,128,1024]{3,2,1,0:T(8,128)} %s_hbm.1, s32[2,1,1,32]{3,2,1,0:T(1,128)} %site_hbm.1, f32[2,2,1,1,32]{4,3,2,1,0:T(1,128)} %via_hbm.1, ...), custom_call_target="tpu_custom_call" | custom-call | tf_op jit(solution)/shard_map/pallas_call | solution.py:548
  14.9 1.6 %shard_map.83 = f32[2,2,128,1024]{3,2,1,0:T(8,128)} custom-call(f32[2,2,8,128,128]{4,3,2,1,0:T(8,128)S(1)} %shard_map.82.cells), custom_call_target="tpu_custom_call" | custom-call | tf_op jit(solution)/shard_map/pallas_call | solution.py:569
